TPU v7x, 32 devices: a whole 2x2x4 slice. The times are simulated.
32 devices in a mesh: fiber: 2 (over x), blk: 16 (over z, y, core).
Axes of the slice: x: 2, y: 2, z: 4, core: 2. Of those that a mesh axis runs over, the one named last changes fastest.
Arguments:
- users: bfloat16 [32768, 256], P('blk', 'fiber'), may hold values from -1.5 to 1.5
- items: bfloat16 [4096, 256], P('blk'), may hold values from -1.5 to 1.5
- tile_users: int32 [16, 2, 128], P('blk', 'fiber'), may hold values from 0 to 15
- tile_items: int32 [16, 2, 128], P('blk', 'fiber'), may hold values from 0 to 31, as said below
- confidence: bfloat16 [16, 2, 128, 128, 128], P('blk', 'fiber'), may hold values from 0.19921875 to 5
Outputs:
- user_grad: bfloat16 [32768, 256], P('blk', 'fiber')
Inputs may be any that keep to these rules, and one draw needn't show every extreme that they name: `tile_items`: each device's list is sorted by item block, then user block, and holds distinct pairs; the two lists of the same index of blk share no pair. A device has at most 8 tiles in any item block, and exactly 8 in at least one.
All inputs are finite; a program needn't handle non-finite values.
Results may differ from a plain program's by a relative error of at most 0.0034.
Values may be sent and summed in bfloat16 or wider, within the bound.
No kernel may reach another device: no remote copies, remote signals or barrier semaphores. Data moves between devices by JAX's collectives and lax.ppermute only.
A program may use at most 128 MiB of HBM per device.

v0:
```python
import math

import jax
import jax.numpy as jnp
from jax import lax
from jax.sharding import PartitionSpec as P


def shards(users, items, tile_users, tile_items, confidence):
    panel_rows = lax.all_gather(users, "fiber", axis=1, tiled=True)
    tile_size = confidence.shape[-1]
    rank_width = panel_rows.shape[1]
    user_count = panel_rows.shape[0] // tile_size
    panel_blocks = panel_rows.reshape(user_count, tile_size, rank_width)
    user_list = tile_users.reshape(-1)
    item_list = tile_items.reshape(-1)
    conf_tiles = confidence.reshape(-1, tile_size, tile_size)
    tile_count = user_list.shape[0]
    item_count = items.shape[0] // tile_size * lax.axis_size("blk")
    block_ids = jnp.arange(user_count, dtype=jnp.int32)

    def accumulate(totals, user_ids, conf_part, item_rows, live_mask):
        user_rows = panel_blocks[user_ids]
        scores = jnp.einsum(
            "tar,tbr->tab", user_rows, item_rows, preferred_element_type=jnp.float32
        )
        weight = (conf_part.astype(jnp.float32) * (1.0 - scores) * live_mask[:, None, None]).astype(
            jnp.bfloat16
        )
        products = jnp.einsum("tab,tbr->tar", weight, item_rows, preferred_element_type=jnp.float32)
        return totals.at[user_ids].add(products)

    empty = jnp.zeros((user_count, tile_size, rank_width), jnp.float32)
    gathered = lax.all_gather(items, "blk", axis=0, tiled=True).reshape(
        item_count, tile_size, rank_width
    )
    group = math.gcd(tile_count, 128)
    every_live = jnp.ones((group,), jnp.float32)

    def one_group(index, running):
        first = (index * group).astype(jnp.int32)
        user_ids = lax.dynamic_slice_in_dim(user_list, first, group, 0)
        item_ids = lax.dynamic_slice_in_dim(item_list, first, group, 0)
        conf_part = lax.dynamic_slice_in_dim(conf_tiles, first, group, 0)
        return accumulate(running, user_ids, conf_part, gathered[item_ids], every_live)

    totals = lax.fori_loop(0, tile_count // group, one_group, empty)
    row_sums = jnp.sum(conf_tiles, axis=-1, dtype=jnp.float32)
    owners = (user_list[:, None] == block_ids[None, :]).astype(jnp.float32)
    row_local = jnp.einsum("tk,ta->ka", owners, row_sums, precision=lax.Precision.HIGHEST).reshape(
        -1
    )
    fiber_count = lax.axis_size("fiber")
    widened = jnp.broadcast_to(row_local[:, None], (row_local.shape[0], fiber_count))
    shares, row_total = (
        lax.psum_scatter(totals.reshape(-1, rank_width), "fiber", scatter_dimension=1, tiled=True),
        lax.psum_scatter(widened, "fiber", scatter_dimension=1, tiled=True),
    )
    return (shares * lax.rsqrt(1.0 + row_total)).astype(jnp.bfloat16)


def solution(mesh):
    in_specs = (
        P("blk", "fiber"),
        P("blk", None),
        P("blk", "fiber", None),
        P("blk", "fiber", None),
        P("blk", "fiber", None, None, None),
    )
    out_specs = P("blk", "fiber")
    return jax.shard_map(shards, mesh=mesh, in_specs=in_specs, out_specs=out_specs, check_vma=False)
```

profile of v0, /device:TPU:0, one launch (start us, length us, event | category | flops | bytes accessed | tf_op | source)
XLA Modules:
  0.0 168.0 jit_solution(1765805471388297682)
XLA Ops:
  6.5 0.0 all-gather.3.cloned.1.call-start
  6.5 0.7 all-gather.3.cloned.1.call-update
  7.3 0.0 all-gather.5.cloned.1.call-start
  7.3 0.7 all-gather.5.cloned.1.call-update
  8.0 0.0 reduce-scatter.2.cloned.1.call-start
  8.1 0.7 fusion.9
  8.7 0.7 fusion.10
  9.4 23.5 %all-gather.3.cloned.1.call-done = bf16[2048,256]{1,0:T(8,128)(2,1)} async-done(((bf16[2048,128]{1,0:T(8,128)(2,1)}), bf16[2048,256]{1,0:T(8,128)(2,1)}) %all-gather.3.cloned.1.call-update) | async-done | bytes 1048592 | tf_op jit(solution)/shard_map/all_gather | solution.py:10
  32.9 7.8 %gather_fusion = bf16[128,128,256]{2,1,0:T(8,128)(2,1)} fusion(bf16[16,128,256]{2,1,0:T(8,128)(2,1)} %bitcast.28, s32[1024]{0:T(1024)S(1)} %pad_clamp_fusion.1), kind=kCustom, calls=%fused_computation | custom fusion | bytes 16777728 | tf_op jit(solution)/shard_map/while/body/eval_jaxpr/gather | solution.py:23
  40.6 35.9 %all-gather.5.cloned.1.call-done = bf16[4096,256]{1,0:T(8,128)(2,1)} async-done(((bf16[256,256]{1,0:T(8,128)(2,1)}), bf16[4096,256]{1,0:T(8,128)(2,1)}) %all-gather.5.cloned.1.call-update) | async-done | bytes 2097168 | tf_op jit(solution)/shard_map/all_gather | solution.py:34
  76.5 8.1 %gather_fusion.1 = bf16[128,128,256]{2,1,0:T(8,128)(2,1)} fusion(bf16[32,128,256]{2,1,0:T(8,128)(2,1)} %bitcast.29, s32[1024]{0:T(1024)S(1)} %pad_clamp_fusion), kind=kCustom, calls=%fused_computation.1 | custom fusion | bytes 16777728 | tf_op jit(solution)/shard_map/while/body/eval_jaxpr/gather | solution.py:45
  84.7 17.4 %fusion.2 = f32[128,128,256]{2,1,0:T(8,128)} fusion(bf16[128,128,256]{2,1,0:T(8,128)(2,1)} %gather_fusion.1, bf16[1,1,128,128,128]{4,3,2,1,0:T(8,128)(2,1)} %param.9, bf16[128,128,256]{2,1,0:T(8,128)(2,1)} %gather_fusion), kind=kOutput, calls=%fused_computation.7 | convolution fusion | flops 2155872256 | bytes 37748736 | tf_op jit(solution)/shard_map/while/body/eval_jaxpr/tab,tbr->tar/dot_general | solution.py:30
  102.1 0.2 broadcast_in_dim.16
  102.3 0.0 copy-start.2
  102.3 0.0 copy-start.1
  102.3 24.3 %scatter_fusion = f32[16,128,256]{2,1,0:T(8,128)S(1)} fusion(f32[16,128,256]{2,1,0:T(8,128)S(1)} %broadcast_in_dim.16, s32[128]{0:T(128)S(1)} %fusion.9, f32[128,128,256]{2,1,0:T(8,128)} %fusion.2), kind=kCustom, calls=%fused_computation.2 | custom fusion | flops 4194304 | bytes 50332160 | tf_op jit(solution)/shard_map/while/body/eval_jaxpr/scatter-add | solution.py:31
  126.6 0.0 copy-start
  126.6 1.3 copy-done
  128.0 0.0 reduce-scatter.2.cloned.1.call-update
  128.0 0.0 copy-done.2
  128.0 0.6 dynamic-slice
  128.6 3.4 %convert_reduce_fusion = f32[128,128]{1,0:T(8,128)S(1)} fusion(bf16[1,1,128,128,128]{4,3,2,1,0:T(8,128)(2,1)} %param.9), kind=kLoop, calls=%fused_computation.3 | loop fusion | flops 4177920 | bytes 4259840 | tf_op jit(solution)/shard_map/reduce_sum | solution.py:48
  132.0 0.0 copy-done.1
  132.0 0.3 convolution_bitcast_fusion
  132.3 8.7 %all-reduce = f32[2048,2]{0,1:T(2,128)S(1)} all-reduce(f32[2048,2]{0,1:T(2,128)S(1)} %broadcast_in_dim.18), channel_id=3, replica_groups=mesh['fiber'=2,'blk'=16] {'fiber'}, use_global_device_ids=true, to_apply=%region_3.0.clone | all-reduce | flops 4096 | bytes 32768
  141.0 0.7 fusion.8
  141.7 17.5 %reduce-scatter.2.cloned.1.call-done = f32[2048,128]{1,0:T(8,128)} async-done(((f32[2048,256]{1,0:T(8,128)}), f32[2048,128]{1,0:T(8,128)}) %reduce-scatter.2.cloned.1.call-update) | async-done | bytes 1048592 | tf_op jit(solution)/shard_map/reduce_scatter | solution.py:56
  159.2 2.4 %multiply_convert_fusion = bf16[2048,128]{1,0:T(8,128)(2,1)} fusion(f32[2048,128]{1,0:T(8,128)} %reduce-scatter.2.cloned.1.call-done, f32[2048]{0:T(1024)S(1)} %bitcast.30), kind=kLoop, calls=%fused_computation.11 | loop fusion | flops 524288 | bytes 1581056 | tf_op jit(solution)/shard_map/convert_element_type | solution.py:59
  (3 shorter events, 0.0 us)
Async XLA Ops:
  6.5 26.3 %all-gather.3.cloned.1.call-start = ((), (), s32[]{:S(2)}) async-start(), calls=%async_computation.1 | async-start | bytes 1572864 | tf_op jit(solution)/shard_map/all_gather | solution.py:10
  7.3 69.3 %all-gather.5.cloned.1.call-start = ((), (), s32[]{:S(2)}) async-start(), calls=%async_computation.2 | async-start | bytes 2228224 | tf_op jit(solution)/shard_map/all_gather | solution.py:34
  8.0 151.2 %reduce-scatter.2.cloned.1.call-start = ((), (), s32[]{:S(2)}) async-start(), calls=%async_computation.3 | async-start | bytes 3145728 | tf_op jit(solution)/shard_map/reduce_scatter | solution.py:56
  102.3 25.7 %copy-start.2 = (u32[32]{0:T(128)S(1)}, u32[32]{0:T(128)}, u32[]{:S(2)}) copy-start(u32[32]{0:T(128)} %constant.29) | copy-start | bytes 388
  102.3 29.7 %copy-start.1 = (s32[1,1,128]{2,1,0:T(1,128)S(1)}, s32[1,1,128]{2,1,0:T(1,128)}, u32[]{:S(2)}) copy-start(s32[1,1,128]{2,1,0:T(1,128)} %param.7) | copy-start | bytes 1540
  126.6 1.3 copy-start
Sparse Core Ops, SparseCore 0:
  8.9 23.9 all-gather.2
  35.0 41.4 all-gather.4
  128.1 31.0 reduce-scatter.1
where the time goes:
time: 169 us; the launch traced here: 168 us
  waiting for transfers between devices  78.3 us (46%)
  other arithmetic  32 us (19%)
  local copies, waits for them, and re-layouts  18.1 us (11%)
  matrix products  17.7 us (10%)
  between operations  13.2 us (8%)
  blocking collectives  8.74 us (5%)
    all_gather x1, waiting for transfers between devices, shards(): lax.all_gather(items, 'blk', axis=0, tiled=True)  35.9 us
    scatter-add x1, other arithmetic, accumulate(): return totals.at[user_ids].add(products)  24.3 us
    all_gather x1, waiting for transfers between devices, shards(): panel_rows = lax.all_gather(users, 'fiber', axis=1, tiled=True)  23.5 us
    reduce_scatter x1, waiting for transfers between devices, shards(): lax.psum_scatter(totals.reshape(-1, rank_width), 'fiber', scatter_dimensi...  17.5 us
    dot_general x1, matrix products, accumulate(): jnp.einsum('tab,tbr->tar', weight, item_rows, preferred_element_type=jnp....  17.4 us
    unnamed x1, blocking collectives  8.74 us
    gather x1, local copies, waits for them, and re-layouts, one_group(): gathered[item_ids]  8.15 us
    gather x1, local copies, waits for them, and re-layouts, accumulate(): user_rows = panel_blocks[user_ids]  7.78 us
  transfers between devices with their start and end apart: 3, of which 3 were waited for; matrix products, arithmetic and copies ran while one was open for 8% of the time, Pallas kernels for 0%

commit v1 on v0

v1 whole, which is shorter than its diff:
```python
import functools

import jax
import jax.numpy as jnp
from jax import lax
from jax.experimental import pallas as pl
from jax.experimental.pallas import tpu as pltpu
from jax.sharding import PartitionSpec as P


F32, BF16, I32 = jnp.float32, jnp.bfloat16, jnp.int32
VM = pl.BlockSpec(memory_space=pltpu.VMEM)
SM = pl.BlockSpec(memory_space=pltpu.SMEM)
STEP = 16
TILE_MIB = 16


def params(mib):
    return pltpu.CompilerParams(vmem_limit_bytes=mib << 20)


def is_late(slot, n_blk):
    return jnp.logical_and((slot & 2) != 0, (slot & (n_blk // 2)) != 0)


def lists(n_blk, per, blocks, users_ref, items_ref, tile_ref, block_ref, slot_ref, count_ref):
    tiles = users_ref.shape[0]
    base = tile_ref.shape[0] // 2
    me = lax.axis_index("blk").astype(I32)

    def body(i, carry):
        a, b = carry
        for j in range(8):
            t = i * 8 + j
            c = items_ref[t]
            slot = lax.div(c, per) ^ me
            hit = is_late(slot, n_blk)
            at = jnp.where(hit, base + b, a)
            tile_ref[at] = t
            block_ref[at] = users_ref[t]
            slot_ref[at] = slot * per + lax.rem(c, per)
            a, b = a + 1 - hit.astype(I32), b + hit.astype(I32)
        return a, b

    a, b = lax.fori_loop(0, tiles // 8, body, (0, 0))
    for start, spare in ((a, 0), (base + b, n_blk * per - 1)):
        for j in range(STEP):
            tile_ref[start + j] = 0
            block_ref[start + j] = blocks
            slot_ref[start + j] = spare
    count_ref[0] = lax.div(a + STEP - 1, STEP)
    count_ref[1] = lax.div(b + STEP - 1, STEP)
    count_ref[2] = lax.axis_index("fiber").astype(I32)


def row_sums(users_ref, conf_ref, mine_ref, items_ref, out_ref, mine_out, items_out, acc_ref):
    mine_out[...] = mine_ref[...]
    items_out[...] = items_ref[...]
    tiles, tb, _ = conf_ref.shape
    blocks = out_ref.shape[0]
    acc_ref[...] = jnp.zeros_like(acc_ref)

    def body(i, _):
        for j in range(4):
            acc_ref[users_ref[i * 4 + j]] += conf_ref[i * 4 + j].astype(F32)
        return 0

    lax.fori_loop(0, tiles // 4, body, 0)
    for k in range(blocks):
        out_ref[k] = jnp.broadcast_to(jnp.sum(acc_ref[k].T, axis=0, keepdims=True), (8, tb))


def scales(mine_ref, other_ref, out_ref):
    blocks, _, tb = mine_ref.shape
    for k in range(blocks):
        row = lax.rsqrt(1.0 + mine_ref[k] + other_ref[k])
        out_ref[k * tb : (k + 1) * tb, :] = jnp.broadcast_to(row[:1, :], (tb, tb)).T


def run_tiles(base, groups, tile_ref, block_ref, slot_ref, full_ref, item_ref, conf_ref, w_ref, acc_ref):
    tb = conf_ref.shape[1]
    last = full_ref.shape[0] // tb - 1

    def rows(block):
        return pl.ds(pl.multiple_of(block * tb, tb), tb)

    def body(g, _):
        first = base + g * STEP
        for j in range(STEP):
            u = full_ref[rows(jnp.minimum(block_ref[first + j], last)), :]
            v = item_ref[slot_ref[first + j]]
            s = lax.dot_general(u, v, (((1,), (1,)), ((), ())), preferred_element_type=F32)
            w_ref[j] = (conf_ref[tile_ref[first + j]].astype(F32) * (1.0 - s)).astype(BF16)
        for j in range(STEP):
            v = item_ref[slot_ref[first + j]]
            acc_ref[rows(block_ref[first + j]), :] += jnp.dot(w_ref[j], v, preferred_element_type=F32)
        return 0

    lax.fori_loop(0, groups, body, 0)


def fill(item_ref, slot_refs, places):
    tb = item_ref.shape[1]
    for s, ref in zip(places, slot_refs):
        per = ref.shape[0] // tb
        for j in range(per):
            item_ref[s * per + j] = ref[j * tb : (j + 1) * tb, :]


def early(places, count_ref, tile_ref, block_ref, slot_ref, mine_ref, other_ref, conf_ref, *refs):
    slot_refs = refs[: len(places)]
    full_ref, acc_ref, item_ref, w_ref = refs[len(places) :]
    half = mine_ref.shape[1]
    here = pl.multiple_of(count_ref[2] * half, half)
    there = pl.multiple_of((1 - count_ref[2]) * half, half)
    full_ref[:, pl.ds(here, half)] = mine_ref[...]
    full_ref[:, pl.ds(there, half)] = other_ref[...]
    fill(item_ref, slot_refs, places)
    acc_ref[...] = jnp.zeros_like(acc_ref)
    run_tiles(0, count_ref[0], tile_ref, block_ref, slot_ref, full_ref, item_ref, conf_ref, w_ref, acc_ref)


def late(places, count_ref, tile_ref, block_ref, slot_ref, full_ref, scale_ref, conf_ref, _, *refs):
    slot_refs = refs[: len(places)]
    keep_ref, send_ref, acc_ref, item_ref, w_ref = refs[len(places) :]
    rows, half = keep_ref.shape
    base = tile_ref.shape[0] // 2
    fill(item_ref, slot_refs, places)
    run_tiles(base, count_ref[1], tile_ref, block_ref, slot_ref, full_ref, item_ref, conf_ref, w_ref, acc_ref)
    here = pl.multiple_of(count_ref[2] * half, half)
    there = pl.multiple_of((1 - count_ref[2]) * half, half)
    send_ref[...] = (acc_ref[:rows, pl.ds(there, half)] * scale_ref[...]).astype(BF16)
    keep_ref[...] = acc_ref[:rows, pl.ds(here, half)] * scale_ref[...]


def gather_items(items, n_blk):
    def swap(x, bits):
        return lax.ppermute(x, "blk", [(i, i ^ bits) for i in range(n_blk)])

    got = {0: items, 2: swap(items, 2)}
    for d in range(4, n_blk, 4):
        low = d & -d
        got[d] = swap(items if d == low else got[d ^ low], d if d == low else low)
    for d in range(4, n_blk, 4):
        got[d | 2] = swap(got[d], 2)
    for d in range(0, n_blk, 2):
        got[d | 1] = swap(got[d], 1)
    return [got[d] for d in range(n_blk)]


def shards(users, items, tile_users, tile_items, confidence):
    n_fiber, n_blk = lax.axis_size("fiber"), lax.axis_size("blk")
    tb = confidence.shape[-1]
    rows, half = users.shape
    blocks = rows // tb
    per = items.shape[0] // tb
    user_list = tile_users.reshape(-1)
    item_list = tile_items.reshape(-1)
    conf = confidence.reshape(-1, tb, tb)
    tiles = conf.shape[0]
    swap_fiber = [(i, n_fiber - 1 - i) for i in range(n_fiber)]
    other = lax.ppermute(users, "fiber", swap_fiber)
    slots = gather_items(items, n_blk)
    entries = jax.ShapeDtypeStruct((2 * (tiles + STEP),), I32)
    tile, block, slot, count = pl.pallas_call(
        functools.partial(lists, n_blk, per, blocks),
        out_shape=(entries, entries, entries, jax.ShapeDtypeStruct((3,), I32)),
        in_specs=[SM, SM],
        out_specs=(SM, SM, SM, SM),
        compiler_params=params(2),
        cost_estimate=pl.CostEstimate(flops=0, bytes_accessed=conf.size * 4, transcendentals=0),
        name="lists",
    )(user_list, item_list)
    sums, mine, slots[0] = pl.pallas_call(
        row_sums,
        out_shape=(
            jax.ShapeDtypeStruct((blocks, 8, tb), F32),
            jax.ShapeDtypeStruct(users.shape, BF16),
            jax.ShapeDtypeStruct(items.shape, BF16),
        ),
        in_specs=[SM, VM, VM, VM],
        out_specs=(VM, VM, VM),
        scratch_shapes=[pltpu.VMEM((blocks, tb, tb), F32)],
        compiler_params=params(4),
        cost_estimate=pl.CostEstimate(flops=0, bytes_accessed=conf.size * 4, transcendentals=0),
        name="sums",
    )(user_list, conf, users, items)
    sums_other = lax.ppermute(sums, "fiber", swap_fiber)
    scale = pl.pallas_call(
        scales,
        out_shape=jax.ShapeDtypeStruct((rows, half), F32),
        in_specs=[VM, VM],
        out_specs=VM,
        compiler_params=params(2),
        name="scales",
    )(sums, sums_other)
    places = ([], [])
    for d in range(n_blk):
        places[bool(d & 2 and d & (n_blk // 2))].append(d)
    scratch = [pltpu.VMEM((n_blk * per, tb, 2 * half), BF16), pltpu.VMEM((STEP, tb, tb), BF16)]
    acc_shape = jax.ShapeDtypeStruct((rows + tb, 2 * half), F32)
    scalars = (count, tile, block, slot)
    full, acc = pl.pallas_call(
        functools.partial(early, places[0]),
        out_shape=(jax.ShapeDtypeStruct((rows, 2 * half), BF16), acc_shape),
        in_specs=[SM] * 4 + [VM] * (3 + len(places[0])),
        out_specs=(VM, VM),
        scratch_shapes=scratch,
        compiler_params=params(TILE_MIB),
        cost_estimate=pl.CostEstimate(flops=tiles * tb * tb * half * 8, bytes_accessed=0, transcendentals=0),
        name="early",
    )(*scalars, mine, other, conf, *[slots[d] for d in places[0]])
    keep, send, _ = pl.pallas_call(
        functools.partial(late, places[1]),
        out_shape=(jax.ShapeDtypeStruct((rows, half), F32), jax.ShapeDtypeStruct((rows, half), BF16), acc_shape),
        in_specs=[SM] * 4 + [VM] * (4 + len(places[1])),
        out_specs=(VM, VM, VM),
        scratch_shapes=scratch,
        input_output_aliases={7: 2},
        compiler_params=params(TILE_MIB),
        name="late",
    )(*scalars, full, scale, conf, acc, *[slots[d] for d in places[1]])
    arrived = lax.ppermute(send, "fiber", swap_fiber)
    return (keep + arrived.astype(F32)).astype(BF16)


def solution(mesh):
    in_specs = (
        P("blk", "fiber"),
        P("blk", None),
        P("blk", "fiber", None),
        P("blk", "fiber", None),
        P("blk", "fiber", None, None, None),
    )
    return jax.shard_map(shards, mesh=mesh, in_specs=in_specs, out_specs=P("blk", "fiber"), check_vma=False)
```

time: 169 us -> 57.2 us (0.34)
  waiting for transfers between devices: 78.3 us -> 24.1 us
  other arithmetic: 32 us -> 0.9 us
  matrix products: 17.7 us -> 0 us
  starting transfers between devices: 0.08 us -> 13.9 us
  local copies, waits for them, and re-layouts: 18.1 us -> 4.79 us
  Pallas kernels: 0 us -> 13.2 us
  between operations: 13.2 us -> 0.1 us
  blocking collectives: 8.74 us -> 0 us
    all_gather x2 -> x0, waiting for transfers between devices: 59.4 us -> none  [the longest x1 35.9 us: shards(): lax.all_gather(items, 'blk', axis=0, tiled=True)]
    scatter-add x1 -> x0, other arithmetic: 24.3 us -> none  [accumulate(): return totals.at[user_ids].add(products)]
    ppermute x0 -> x18, waiting for transfers between devices: none -> 24.1 us  [the longest x1 12.9 us: shards(): arrived = lax.ppermute(send, 'fiber', swap_fiber)]
    dot_general x2 -> x0, matrix products: 17.7 us -> none  [the longest x1 17.4 us: accumulate(): jnp.einsum('tab,tbr->tar', weight, item_rows, preferred_element_type=jnp....]
    reduce_scatter x1 -> x0, waiting for transfers between devices: 17.5 us -> none  [shards(): lax.psum_scatter(totals.reshape(-1, rank_width), 'fiber', scatter_dimensi...]
    gather x2 -> x0, local copies, waits for them, and re-layouts: 15.9 us -> none  [the longest x1 8.15 us: one_group(): gathered[item_ids]]
    ppermute x0 -> x18, starting transfers between devices: none -> 13.9 us  [the longest x15 10.4 us: swap(): return lax.ppermute(x, 'blk', [(i, i ^ bits) for i in range(n_blk)])]
    pallas_call x0 -> x5, Pallas kernels: none -> 13.2 us  [the longest x1 6.12 us: shards(): pl.pallas_call(functools.partial(early, places[0]), out_shape=(jax.ShapeD...]
  transfers between devices with their start and end apart: 3 -> 18, of which waited for: 3 -> 7; matrix products, arithmetic and copies ran while one was open for 8% -> 0% of each run, Pallas kernels for 0% -> 19%
where the time goes in v1:
time: 57.2 us; the launch traced here: 57 us
  waiting for transfers between devices  24.1 us (42%)
  starting transfers between devices  13.9 us (24%)
  Pallas kernels  13.2 us (23%)
  local copies, waits for them, and re-layouts  4.79 us (8%)
  other arithmetic  0.9 us (2%)
    ppermute x1, waiting for transfers between devices, shards(): arrived = lax.ppermute(send, 'fiber', swap_fiber)  12.9 us
    ppermute x15, starting transfers between devices, swap(): return lax.ppermute(x, 'blk', [(i, i ^ bits) for i in range(n_blk)])  10.4 us
    ppermute x15, waiting for transfers between devices, swap(): return lax.ppermute(x, 'blk', [(i, i ^ bits) for i in range(n_blk)])  7.61 us
    pallas_call x1, Pallas kernels, shards(): pl.pallas_call(functools.partial(early, places[0]), out_shape=(jax.ShapeD...  6.12 us
    unnamed x12, local copies, waits for them, and re-layouts  4.79 us
    ppermute x1, waiting for transfers between devices, shards(): sums_other = lax.ppermute(sums, 'fiber', swap_fiber)  3.56 us
    pallas_call x1, Pallas kernels, shards(): pl.pallas_call(functools.partial(lists, n_blk, per, blocks), out_shape=(e...  2.42 us
    pallas_call x1, Pallas kernels, shards(): pl.pallas_call(functools.partial(late, places[1]), out_shape=(jax.ShapeDt...  2.34 us
  transfers between devices with their start and end apart: 18, of which 7 were waited for; matrix products, arithmetic and copies ran while one was open for 0% of the time, Pallas kernels for 19%

profile of v1, /device:TPU:0, one launch (start us, length us, event | category | flops | bytes accessed | tf_op | source)
XLA Modules:
  0.0 57.0 jit_solution(17801614398935860397)
XLA Ops:
  0.0 3.0 %collective-permute-start.2 = (bf16[256,256]{1,0:T(8,128)(2,1)}, bf16[256,256]{1,0:T(8,128)(2,1)S(1)}, u32[]{:S(2)}, u32[]{:S(2)}) collective-permute-start(bf16[256,256]{1,0:T(8,128)(2,1)} %items_ref.1), channel_id=1, source_target_pairs={{0,2},{1,3},{2,0},{3,1},{4,6},{5,7},{6,4},{7,5},{8,10},{9,11},{10,... | collective-permute-start | bytes 393224 | tf_op jit(solution)/shard_map/ppermute | solution.py:138
  3.0 1.5 %collective-permute-start = (bf16[2048,128]{1,0:T(8,128)(2,1)}, bf16[2048,128]{1,0:T(8,128)(2,1)S(1)}, u32[]{:S(2)}, u32[]{:S(2)}) collective-permute-start(bf16[2048,128]{1,0:T(8,128)(2,1)} %mine_ref.1), channel_id=1, source_target_pairs={{0,16},{16,0},{1,17},{17,1},{2,18},{18,2},{3,19},{19,3},{4,20},{20... | collective-permute-start | bytes 1572872 | tf_op jit(solution)/shard_map/ppermute | solution.py:162
  4.5 0.0 copy-start
  4.5 2.2 %copy-done = bf16[1,1,128,128,128]{4,3,2,1,0:T(8,128)(2,1)S(1)} copy-done((bf16[1,1,128,128,128]{4,3,2,1,0:T(8,128)(2,1)S(1)}, bf16[1,1,128,128,128]{4,3,2,1,0:T(8,128)(2,1)}, u32[]{:S(2)}) %copy-start) | copy-done | bytes 4194328
  6.7 0.0 copy-start.2
  6.7 1.0 %copy-done.2 = bf16[2048,128]{1,0:T(8,128)(2,1)S(1)} copy-done((bf16[2048,128]{1,0:T(8,128)(2,1)S(1)}, bf16[2048,128]{1,0:T(8,128)(2,1)}, u32[]{:S(2)}) %copy-start.2) | copy-done | bytes 524312
  7.7 0.0 copy-start.3
  7.7 0.9 %copy-done.3 = bf16[256,256]{1,0:T(8,128)(2,1)S(1)} copy-done((bf16[256,256]{1,0:T(8,128)(2,1)S(1)}, bf16[256,256]{1,0:T(8,128)(2,1)}, u32[]{:S(2)}) %copy-start.3) | copy-done | bytes 131096
  8.6 0.0 copy-start.4
  8.6 0.7 %copy-done.4 = s32[1,1,128]{2,1,0:T(1,128)S(1)} copy-done((s32[1,1,128]{2,1,0:T(1,128)S(1)}, s32[1,1,128]{2,1,0:T(1,128)}, u32[]{:S(2)}) %copy-start.4) | copy-done | bytes 536
  9.3 0.0 copy-start.5
  9.3 0.0 copy-start.1
  9.3 1.9 %sums.1 = (f32[16,8,128]{2,1,0:T(8,128)S(1)}, bf16[2048,128]{1,0:T(8,128)(2,1)S(1)}, bf16[256,256]{1,0:T(8,128)(2,1)S(1)}) custom-call(s32[128]{0:T(128)S(1)} %bitcast.6, bf16[128,128,128]{2,1,0:T(8,128)(2,1)S(1)} %bitcast.3, bf16[2048,128]{1,0:T(8,128)(2,1)S(1)} %copy-done.2, bf16[256,256]{1,0:T(8,128)(2,1)S(1)} %copy-done.3), custom_call_target="tpu_custom_call" | custom-call | bytes 8388608 | tf_op jit(solution)/shard_map/sums/pallas_call | solution.py:174
  11.2 0.6 %collective-permute-start.12 = (f32[16,8,128]{2,1,0:T(8,128)S(1)}, f32[16,8,128]{2,1,0:T(8,128)S(1)}, u32[]{:S(2)}, u32[]{:S(2)}) collective-permute-start(f32[16,8,128]{2,1,0:T(8,128)S(1)} %get-tuple-element.23.mine_ref), channel_id=1, source_target_pairs={{0,16},{16,0},{1,17},{17,1},{2,18},{18,2},{3,19},{19,3},{4,20},{20... | collective-permute-start | bytes 196616 | tf_op jit(solution)/shard_map/ppermute | solution.py:188
  11.8 2.6 %collective-permute-start.8 = (bf16[256,256]{1,0:T(8,128)(2,1)S(1)}, bf16[256,256]{1,0:T(8,128)(2,1)S(1)}, u32[]{:S(2)}, u32[]{:S(2)}) collective-permute-start(bf16[256,256]{1,0:T(8,128)(2,1)S(1)} %copy-done.3), channel_id=1, source_target_pairs={{0,8},{1,9},{2,10},{3,11},{4,12},{5,13},{6,14},{7,15},{8,0},{9,1},... | collective-permute-start | bytes 393224 | tf_op jit(solution)/shard_map/ppermute | solution.py:138
  14.4 0.0 collective-permute-start.1
  14.4 3.6 %collective-permute-done.12.other_ref = f32[16,8,128]{2,1,0:T(8,128)S(1)} collective-permute-done((f32[16,8,128]{2,1,0:T(8,128)S(1)}, f32[16,8,128]{2,1,0:T(8,128)S(1)}, u32[]{:S(2)}, u32[]{:S(2)}) %collective-permute-start.12) | collective-permute-done | bytes 65568 | tf_op jit(solution)/shard_map/ppermute | solution.py:188
  18.0 1.6 %collective-permute-start.4 = (bf16[256,256]{1,0:T(8,128)(2,1)S(1)}, bf16[256,256]{1,0:T(8,128)(2,1)S(1)}, u32[]{:S(2)}, u32[]{:S(2)}) collective-permute-start(bf16[256,256]{1,0:T(8,128)(2,1)S(1)} %copy-done.3), channel_id=1, source_target_pairs={{0,4},{1,5},{2,6},{3,7},{4,0},{5,1},{6,2},{7,3},{8,12},{9,13},{10,... | collective-permute-start | bytes 393224 | tf_op jit(solution)/shard_map/ppermute | solution.py:138
  19.6 0.0 collective-permute-done.2.refs_2_
  19.6 0.0 collective-permute-start.3
  19.6 0.4 collective-permute-done.8.refs_8_
  20.0 0.4 collective-permute-start.13
  20.5 0.0 collective-permute-done.1.refs_1_
  20.5 0.7 %collective-permute-start.10 = (bf16[256,256]{1,0:T(8,128)(2,1)S(1)}, bf16[256,256]{1,0:T(8,128)(2,1)S(1)}, u32[]{:S(2)}, u32[]{:S(2)}) collective-permute-start(bf16[256,256]{1,0:T(8,128)(2,1)S(1)} %collective-permute-done.8.refs_8_), channel_id=1, source_target_pairs={{0,4},{1,5},{2,6},{3,7},{4,0},{5,1},{6,2},{7,3},{8,12},{9,13},{10,... | collective-permute-start | bytes 393224 | tf_op jit(solution)/shard_map/ppermute | solution.py:138
  21.1 2.3 %collective-permute-done.4.refs_4_ = bf16[256,256]{1,0:T(8,128)(2,1)S(1)} collective-permute-done((bf16[256,256]{1,0:T(8,128)(2,1)S(1)}, bf16[256,256]{1,0:T(8,128)(2,1)S(1)}, u32[]{:S(2)}, u32[]{:S(2)}) %collective-permute-start.4) | collective-permute-done | bytes 131104 | tf_op jit(solution)/shard_map/ppermute | solution.py:138
  23.4 0.0 collective-permute-start.9
  23.4 0.0 collective-permute-done.3.refs_3_
  23.4 0.0 collective-permute-start.6
  23.4 2.1 %collective-permute-done.13.refs_0_ = bf16[256,256]{1,0:T(8,128)(2,1)S(1)} collective-permute-done((bf16[256,256]{1,0:T(8,128)(2,1)S(1)}, bf16[256,256]{1,0:T(8,128)(2,1)S(1)}, u32[]{:S(2)}, u32[]{:S(2)}) %collective-permute-start.13) | collective-permute-done | bytes 131104 | tf_op jit(solution)/shard_map/ppermute | solution.py:138
  25.5 0.0 collective-permute-start.5
  25.5 0.3 collective-permute-done.10.refs_10_
  25.8 1.5 %collective-permute-start.15 = (bf16[256,256]{1,0:T(8,128)(2,1)S(1)}, bf16[256,256]{1,0:T(8,128)(2,1)S(1)}, u32[]{:S(2)}, u32[]{:S(2)}) collective-permute-start(bf16[256,256]{1,0:T(8,128)(2,1)S(1)} %collective-permute-done.10.refs_10_), channel_id=1, source_target_pairs={{0,2},{1,3},{2,0},{3,1},{4,6},{5,7},{6,4},{7,5},{8,10},{9,11},{10,... | collective-permute-start | bytes 393224 | tf_op jit(solution)/shard_map/ppermute | solution.py:138
  27.2 0.0 collective-permute-done.9.refs_9_
  27.2 0.0 collective-permute-start.11
  27.2 2.5 %collective-permute-done.6.refs_6_ = bf16[256,256]{1,0:T(8,128)(2,1)S(1)} collective-permute-done((bf16[256,256]{1,0:T(8,128)(2,1)S(1)}, bf16[256,256]{1,0:T(8,128)(2,1)S(1)}, u32[]{:S(2)}, u32[]{:S(2)}) %collective-permute-start.6) | collective-permute-done | bytes 131104 | tf_op jit(solution)/shard_map/ppermute | solution.py:138
  29.8 0.0 collective-permute-start.7
  29.8 0.0 copy-done.5
  29.8 2.4 %lists.1 = (s32[288]{0:T(512)S(1)}, s32[288]{0:T(512)S(1)}, s32[288]{0:T(512)S(1)}, s32[3]{0:T(128)S(1)}) custom-call(s32[128]{0:T(128)S(1)} %bitcast.7, s32[128]{0:T(128)S(1)} %bitcast.8), custom_call_target="tpu_custom_call" | custom-call | bytes 8388608 | tf_op jit(solution)/shard_map/lists/pallas_call | solution.py:165
  32.2 0.3 scales.1.scale_ref
  32.5 0.0 collective-permute-done.5.refs_5_
  32.6 0.6 %collective-permute-start.14 = (bf16[256,256]{1,0:T(8,128)(2,1)S(1)}, bf16[256,256]{1,0:T(8,128)(2,1)S(1)}, u32[]{:S(2)}, u32[]{:S(2)}) collective-permute-start(bf16[256,256]{1,0:T(8,128)(2,1)S(1)} %collective-permute-done.13.refs_0_), channel_id=1, source_target_pairs={{0,1},{1,0},{2,3},{3,2},{4,5},{5,4},{6,7},{7,6},{8,9},{9,8},{10,11... | collective-permute-start | bytes 393224 | tf_op jit(solution)/shard_map/ppermute | solution.py:138
  33.1 0.0 collective-permute-done.15.refs_2_
  33.1 0.1 collective-permute-start.16
  33.2 0.0 collective-permute-done.11.refs_11_
  33.2 0.0 collective-permute-done.7.refs_7_
  33.2 0.0 collective-permute-done.other_ref
  33.2 0.0 copy-done.1
  33.2 6.1 %early.1 = (bf16[2048,256]{1,0:T(8,128)(2,1)S(1)}, f32[2176,256]{1,0:T(8,128)S(1)}) custom-call(s32[3]{0:T(128)S(1)} %get-tuple-element.16.count_ref, s32[288]{0:T(512)S(1)} %get-tuple-element.17.tile_ref, s32[288]{0:T(512)S(1)} %get-tuple-element.18.block_ref, s32[288]{0:T(512)S(1)} %get-tuple-element.19.slot_ref, ...), custom_call_target="tpu_custom_call" | custom-call | flops 2147483648 | tf_op jit(solution)/shard_map/early/pallas_call | solution.py:203
  39.4 0.0 collective-permute-done.14.refs_1_
  39.4 0.0 collective-permute-done.16.refs_3_
  39.4 2.3 %late.1 = (f32[2048,128]{1,0:T(8,128)S(1)}, bf16[2048,128]{1,0:T(8,128)(2,1)S(1)}, f32[2176,256]{1,0:T(8,128)S(1)}) custom-call(s32[3]{0:T(128)S(1)} %get-tuple-element.16.count_ref, s32[288]{0:T(512)S(1)} %get-tuple-element.17.tile_ref, s32[288]{0:T(512)S(1)} %get-tuple-element.18.block_ref, ...), custom_call_target="tpu_custom_call", output_to_operand_aliasing={{2}: (7, {})} | custom-call | tf_op jit(solution)/shard_map/late/pallas_call | solution.py:213
  41.7 1.4 %collective-permute-start.17 = (bf16[2048,128]{1,0:T(8,128)(2,1)S(1)}, bf16[2048,128]{1,0:T(8,128)(2,1)S(1)}, u32[]{:S(2)}, u32[]{:S(2)}) collective-permute-start(bf16[2048,128]{1,0:T(8,128)(2,1)S(1)} %get-tuple-element.26), channel_id=1, source_target_pairs={{0,16},{16,0},{1,17},{17,1},{2,18},{18,2},{3,19},{19,3},{4,20},{20... | collective-permute-start | bytes 1572872 | tf_op jit(solution)/shard_map/ppermute | solution.py:223
  43.1 12.9 %collective-permute-done.17 = bf16[2048,128]{1,0:T(8,128)(2,1)S(1)} collective-permute-done((bf16[2048,128]{1,0:T(8,128)(2,1)S(1)}, bf16[2048,128]{1,0:T(8,128)(2,1)S(1)}, u32[]{:S(2)}, u32[]{:S(2)}) %collective-permute-start.17) | collective-permute-done | bytes 524320 | tf_op jit(solution)/shard_map/ppermute | solution.py:223
  56.1 0.9 %add_convert_fusion = bf16[2048,128]{1,0:T(8,128)(2,1)} fusion(f32[2048,128]{1,0:T(8,128)S(1)} %get-tuple-element.25, bf16[2048,128]{1,0:T(8,128)(2,1)S(1)} %collective-permute-done.17), kind=kLoop, calls=%fused_computation | loop fusion | flops 786432 | bytes 2097152 | tf_op jit(solution)/shard_map/convert_element_type | solution.py:224
Async XLA Ops:
  0.0 19.6 %collective-permute-start.2 = (bf16[256,256]{1,0:T(8,128)(2,1)}, bf16[256,256]{1,0:T(8,128)(2,1)S(1)}, u32[]{:S(2)}, u32[]{:S(2)}) collective-permute-start(bf16[256,256]{1,0:T(8,128)(2,1)} %items_ref.1), channel_id=1, source_target_pairs={{0,2},{1,3},{2,0},{3,1},{4,6},{5,7},{6,4},{7,5},{8,10},{9,11},{10,... | collective-permute-start | bytes 393224 | tf_op jit(solution)/shard_map/ppermute | solution.py:138
  3.0 30.2 %collective-permute-start = (bf16[2048,128]{1,0:T(8,128)(2,1)}, bf16[2048,128]{1,0:T(8,128)(2,1)S(1)}, u32[]{:S(2)}, u32[]{:S(2)}) collective-permute-start(bf16[2048,128]{1,0:T(8,128)(2,1)} %mine_ref.1), channel_id=1, source_target_pairs={{0,16},{16,0},{1,17},{17,1},{2,18},{18,2},{3,19},{19,3},{4,20},{20... | collective-permute-start | bytes 1572872 | tf_op jit(solution)/shard_map/ppermute | solution.py:162
  4.5 2.2 %copy-start = (bf16[1,1,128,128,128]{4,3,2,1,0:T(8,128)(2,1)S(1)}, bf16[1,1,128,128,128]{4,3,2,1,0:T(8,128)(2,1)}, u32[]{:S(2)}) copy-start(bf16[1,1,128,128,128]{4,3,2,1,0:T(8,128)(2,1)} %param.9) | copy-start | bytes 12582916
  6.7 1.0 %copy-start.2 = (bf16[2048,128]{1,0:T(8,128)(2,1)S(1)}, bf16[2048,128]{1,0:T(8,128)(2,1)}, u32[]{:S(2)}) copy-start(bf16[2048,128]{1,0:T(8,128)(2,1)} %mine_ref.1) | copy-start | bytes 1572868
  7.7 0.9 %copy-start.3 = (bf16[256,256]{1,0:T(8,128)(2,1)S(1)}, bf16[256,256]{1,0:T(8,128)(2,1)}, u32[]{:S(2)}) copy-start(bf16[256,256]{1,0:T(8,128)(2,1)} %items_ref.1) | copy-start | bytes 393220
  8.6 0.7 %copy-start.4 = (s32[1,1,128]{2,1,0:T(1,128)S(1)}, s32[1,1,128]{2,1,0:T(1,128)}, u32[]{:S(2)}) copy-start(s32[1,1,128]{2,1,0:T(1,128)} %param.7) | copy-start | bytes 1540
  9.3 20.5 %copy-start.5 = (s32[1,1,128]{2,1,0:T(1,128)S(1)}, s32[1,1,128]{2,1,0:T(1,128)}, u32[]{:S(2)}) copy-start(s32[1,1,128]{2,1,0:T(1,128)} %param.8) | copy-start | bytes 1540
  9.3 24.0 %copy-start.1 = (bf16[1,1,128,128,128]{4,3,2,1,0:T(8,128)(2,1)S(1)}, bf16[1,1,128,128,128]{4,3,2,1,0:T(8,128)(2,1)}, u32[]{:S(2)}) copy-start(bf16[1,1,128,128,128]{4,3,2,1,0:T(8,128)(2,1)} %param.9) | copy-start | bytes 12582916
  11.2 6.8 %collective-permute-start.12 = (f32[16,8,128]{2,1,0:T(8,128)S(1)}, f32[16,8,128]{2,1,0:T(8,128)S(1)}, u32[]{:S(2)}, u32[]{:S(2)}) collective-permute-start(f32[16,8,128]{2,1,0:T(8,128)S(1)} %get-tuple-element.23.mine_ref), channel_id=1, source_target_pairs={{0,16},{16,0},{1,17},{17,1},{2,18},{18,2},{3,19},{19,3},{4,20},{20... | collective-permute-start | bytes 196616 | tf_op jit(solution)/shard_map/ppermute | solution.py:188
  11.8 8.2 %collective-permute-start.8 = (bf16[256,256]{1,0:T(8,128)(2,1)S(1)}, bf16[256,256]{1,0:T(8,128)(2,1)S(1)}, u32[]{:S(2)}, u32[]{:S(2)}) collective-permute-start(bf16[256,256]{1,0:T(8,128)(2,1)S(1)} %copy-done.3), channel_id=1, source_target_pairs={{0,8},{1,9},{2,10},{3,11},{4,12},{5,13},{6,14},{7,15},{8,0},{9,1},... | collective-permute-start | bytes 393224 | tf_op jit(solution)/shard_map/ppermute | solution.py:138
  14.4 6.0 %collective-permute-start.1 = (bf16[256,256]{1,0:T(8,128)(2,1)S(1)}, bf16[256,256]{1,0:T(8,128)(2,1)S(1)}, u32[]{:S(2)}, u32[]{:S(2)}) collective-permute-start(bf16[256,256]{1,0:T(8,128)(2,1)S(1)} %copy-done.3), channel_id=1, source_target_pairs={{0,1},{1,0},{2,3},{3,2},{4,5},{5,4},{6,7},{7,6},{8,9},{9,8},{10,11... | collective-permute-start | bytes 393224 | tf_op jit(solution)/shard_map/ppermute | solution.py:138
  18.0 5.4 %collective-permute-start.4 = (bf16[256,256]{1,0:T(8,128)(2,1)S(1)}, bf16[256,256]{1,0:T(8,128)(2,1)S(1)}, u32[]{:S(2)}, u32[]{:S(2)}) collective-permute-start(bf16[256,256]{1,0:T(8,128)(2,1)S(1)} %copy-done.3), channel_id=1, source_target_pairs={{0,4},{1,5},{2,6},{3,7},{4,0},{5,1},{6,2},{7,3},{8,12},{9,13},{10,... | collective-permute-start | bytes 393224 | tf_op jit(solution)/shard_map/ppermute | solution.py:138
  19.6 3.8 %collective-permute-start.3 = (bf16[256,256]{1,0:T(8,128)(2,1)S(1)}, bf16[256,256]{1,0:T(8,128)(2,1)S(1)}, u32[]{:S(2)}, u32[]{:S(2)}) collective-permute-start(bf16[256,256]{1,0:T(8,128)(2,1)S(1)} %collective-permute-done.2.refs_2_), channel_id=1, source_target_pairs={{0,1},{1,0},{2,3},{3,2},{4,5},{5,4},{6,7},{7,6},{8,9},{9,8},{10,11... | collective-permute-start | bytes 393224 | tf_op jit(solution)/shard_map/ppermute | solution.py:138
  20.0 5.5 %collective-permute-start.13 = (bf16[256,256]{1,0:T(8,128)(2,1)S(1)}, bf16[256,256]{1,0:T(8,128)(2,1)S(1)}, u32[]{:S(2)}, u32[]{:S(2)}) collective-permute-start(bf16[256,256]{1,0:T(8,128)(2,1)S(1)} %collective-permute-done.8.refs_8_), channel_id=1, source_target_pairs={{0,2},{1,3},{2,0},{3,1},{4,6},{5,7},{6,4},{7,5},{8,10},{9,11},{10,... | collective-permute-start | bytes 393224 | tf_op jit(solution)/shard_map/ppermute | solution.py:138
  20.5 5.3 %collective-permute-start.10 = (bf16[256,256]{1,0:T(8,128)(2,1)S(1)}, bf16[256,256]{1,0:T(8,128)(2,1)S(1)}, u32[]{:S(2)}, u32[]{:S(2)}) collective-permute-start(bf16[256,256]{1,0:T(8,128)(2,1)S(1)} %collective-permute-done.8.refs_8_), channel_id=1, source_target_pairs={{0,4},{1,5},{2,6},{3,7},{4,0},{5,1},{6,2},{7,3},{8,12},{9,13},{10,... | collective-permute-start | bytes 393224 | tf_op jit(solution)/shard_map/ppermute | solution.py:138
  23.4 3.9 %collective-permute-start.9 = (bf16[256,256]{1,0:T(8,128)(2,1)S(1)}, bf16[256,256]{1,0:T(8,128)(2,1)S(1)}, u32[]{:S(2)}, u32[]{:S(2)}) collective-permute-start(bf16[256,256]{1,0:T(8,128)(2,1)S(1)} %collective-permute-done.8.refs_8_), channel_id=1, source_target_pairs={{0,1},{1,0},{2,3},{3,2},{4,5},{5,4},{6,7},{7,6},{8,9},{9,8},{10,11... | collective-permute-start | bytes 393224 | tf_op jit(solution)/shard_map/ppermute | solution.py:138
  23.4 6.4 %collective-permute-start.6 = (bf16[256,256]{1,0:T(8,128)(2,1)S(1)}, bf16[256,256]{1,0:T(8,128)(2,1)S(1)}, u32[]{:S(2)}, u32[]{:S(2)}) collective-permute-start(bf16[256,256]{1,0:T(8,128)(2,1)S(1)} %collective-permute-done.4.refs_4_), channel_id=1, source_target_pairs={{0,2},{1,3},{2,0},{3,1},{4,6},{5,7},{6,4},{7,5},{8,10},{9,11},{10,... | collective-permute-start | bytes 393224 | tf_op jit(solution)/shard_map/ppermute | solution.py:138
  25.5 7.1 %collective-permute-start.5 = (bf16[256,256]{1,0:T(8,128)(2,1)S(1)}, bf16[256,256]{1,0:T(8,128)(2,1)S(1)}, u32[]{:S(2)}, u32[]{:S(2)}) collective-permute-start(bf16[256,256]{1,0:T(8,128)(2,1)S(1)} %collective-permute-done.4.refs_4_), channel_id=1, source_target_pairs={{0,1},{1,0},{2,3},{3,2},{4,5},{5,4},{6,7},{7,6},{8,9},{9,8},{10,11... | collective-permute-start | bytes 393224 | tf_op jit(solution)/shard_map/ppermute | solution.py:138
  25.8 7.4 %collective-permute-start.15 = (bf16[256,256]{1,0:T(8,128)(2,1)S(1)}, bf16[256,256]{1,0:T(8,128)(2,1)S(1)}, u32[]{:S(2)}, u32[]{:S(2)}) collective-permute-start(bf16[256,256]{1,0:T(8,128)(2,1)S(1)} %collective-permute-done.10.refs_10_), channel_id=1, source_target_pairs={{0,2},{1,3},{2,0},{3,1},{4,6},{5,7},{6,4},{7,5},{8,10},{9,11},{10,... | collective-permute-start | bytes 393224 | tf_op jit(solution)/shard_map/ppermute | solution.py:138
  27.2 6.0 %collective-permute-start.11 = (bf16[256,256]{1,0:T(8,128)(2,1)S(1)}, bf16[256,256]{1,0:T(8,128)(2,1)S(1)}, u32[]{:S(2)}, u32[]{:S(2)}) collective-permute-start(bf16[256,256]{1,0:T(8,128)(2,1)S(1)} %collective-permute-done.10.refs_10_), channel_id=1, source_target_pairs={{0,1},{1,0},{2,3},{3,2},{4,5},{5,4},{6,7},{7,6},{8,9},{9,8},{10,11... | collective-permute-start | bytes 393224 | tf_op jit(solution)/shard_map/ppermute | solution.py:138
  29.8 3.5 %collective-permute-start.7 = (bf16[256,256]{1,0:T(8,128)(2,1)S(1)}, bf16[256,256]{1,0:T(8,128)(2,1)S(1)}, u32[]{:S(2)}, u32[]{:S(2)}) collective-permute-start(bf16[256,256]{1,0:T(8,128)(2,1)S(1)} %collective-permute-done.6.refs_6_), channel_id=1, source_target_pairs={{0,1},{1,0},{2,3},{3,2},{4,5},{5,4},{6,7},{7,6},{8,9},{9,8},{10,11... | collective-permute-start | bytes 393224 | tf_op jit(solution)/shard_map/ppermute | solution.py:138
  32.6 6.8 %collective-permute-start.14 = (bf16[256,256]{1,0:T(8,128)(2,1)S(1)}, bf16[256,256]{1,0:T(8,128)(2,1)S(1)}, u32[]{:S(2)}, u32[]{:S(2)}) collective-permute-start(bf16[256,256]{1,0:T(8,128)(2,1)S(1)} %collective-permute-done.13.refs_0_), channel_id=1, source_target_pairs={{0,1},{1,0},{2,3},{3,2},{4,5},{5,4},{6,7},{7,6},{8,9},{9,8},{10,11... | collective-permute-start | bytes 393224 | tf_op jit(solution)/shard_map/ppermute | solution.py:138
  33.1 6.2 %collective-permute-start.16 = (bf16[256,256]{1,0:T(8,128)(2,1)S(1)}, bf16[256,256]{1,0:T(8,128)(2,1)S(1)}, u32[]{:S(2)}, u32[]{:S(2)}) collective-permute-start(bf16[256,256]{1,0:T(8,128)(2,1)S(1)} %collective-permute-done.15.refs_2_), channel_id=1, source_target_pairs={{0,1},{1,0},{2,3},{3,2},{4,5},{5,4},{6,7},{7,6},{8,9},{9,8},{10,11... | collective-permute-start | bytes 393224 | tf_op jit(solution)/shard_map/ppermute | solution.py:138
  41.7 14.3 %collective-permute-start.17 = (bf16[2048,128]{1,0:T(8,128)(2,1)S(1)}, bf16[2048,128]{1,0:T(8,128)(2,1)S(1)}, u32[]{:S(2)}, u32[]{:S(2)}) collective-permute-start(bf16[2048,128]{1,0:T(8,128)(2,1)S(1)} %get-tuple-element.26), channel_id=1, source_target_pairs={{0,16},{16,0},{1,17},{17,1},{2,18},{18,2},{3,19},{19,3},{4,20},{20... | collective-permute-start | bytes 1572872 | tf_op jit(solution)/shard_map/ppermute | solution.py:223

commit v2 on v1

v2 whole, which is shorter than its diff:
```python
import functools

import jax
import jax.numpy as jnp
from jax import lax
from jax.experimental import pallas as pl
from jax.experimental.pallas import tpu as pltpu
from jax.sharding import PartitionSpec as P


F32, BF16, I32 = jnp.float32, jnp.bfloat16, jnp.int32
VM = pl.BlockSpec(memory_space=pltpu.VMEM)
HBM = pl.BlockSpec(memory_space=pltpu.HBM)
SM = pl.BlockSpec(memory_space=pltpu.SMEM)
STEP = 16
UNROLL = 16
SLOT_BITS, BLOCK_BITS = 10, 8
TILE_MIB = 16


def params(mib):
    return pltpu.CompilerParams(vmem_limit_bytes=mib << 20)


def stage_of(slot, n_blk):
    chip = slot >> 1
    one = (chip & (chip - 1)) == 0
    return jnp.where(one, 0, jnp.where(chip == n_blk // 2 - 1, 2, 1))


def prepare(n_blk, per, spare, users_hbm, items_hbm, conf_hbm, mine_hbm, own_hbm, sums_ref, conf_ref, mine_ref, own_ref, list_ref, count_ref, users_ref, items_ref, table_ref, ends_ref, acc_ref, sems):
    tiles, _, _ = conf_ref.shape
    blocks = sums_ref.shape[0]
    parts = sems.shape[0] - 4
    part = tiles // parts
    base = list_ref.shape[0] // 4
    me = lax.axis_index("blk").astype(I32)

    def conf_copy(i):
        at = pl.ds(i * part, part)
        return pltpu.make_async_copy(conf_hbm.at[at], conf_ref.at[at], sems.at[i])

    def other_copy(src, dst, i):
        return pltpu.make_async_copy(src, dst, sems.at[parts + i])

    first = [other_copy(users_hbm, users_ref, 0), other_copy(items_hbm, items_ref, 1)]
    later = [other_copy(mine_hbm, mine_ref, 2), other_copy(own_hbm, own_ref, 3)]
    for c in first:
        c.start()
    for i in range(parts):
        conf_copy(i).start()
    for c in later:
        c.start()
    acc_ref[...] = jnp.zeros_like(acc_ref)
    for item in range(table_ref.shape[0]):
        slot = item // per ^ me
        table_ref[item] = (stage_of(slot, n_blk) << SLOT_BITS) + slot * per + item % per
    for i in range(4):
        ends_ref[i] = i * base
    for c in first:
        c.wait()

    def body(i, _):
        conf_copy(i).wait()

        def inner(j, _):
            for k in range(UNROLL):
                t = i * part + j * UNROLL + k
                user, found = users_ref[t], table_ref[items_ref[t]]
                stage = jnp.where(user >= blocks // 2, 3, found >> SLOT_BITS)
                end = ends_ref[stage]
                ends_ref[stage] = end + 1
                list_ref[end] = ((t << BLOCK_BITS) + user << SLOT_BITS) + (found & ((1 << SLOT_BITS) - 1))
                acc_ref[user] += conf_ref[t].astype(F32)
            return 0

        return lax.fori_loop(0, part // UNROLL, inner, 0)

    lax.fori_loop(0, parts, body, 0)
    ends = [ends_ref[i] for i in range(4)]
    spares = ((blocks // 2, 0), (blocks // 2, spare * per), (blocks // 2, n_blk * per - 1), (blocks, 0))
    for i, (end, (block, slot)) in enumerate(zip(ends, spares)):
        for j in range(STEP):
            list_ref[end + j] = (block << SLOT_BITS) + slot
        count_ref[i] = lax.div(end - i * base + STEP - 1, STEP)
    count_ref[4] = lax.axis_index("fiber").astype(I32)
    for k in range(blocks):
        sums_ref[k : k + 1, :] = jnp.sum(acc_ref[k].T, axis=0, keepdims=True)
    for c in later:
        c.wait()


def scales(mine_ref, other_ref, out_ref):
    blocks, tb = mine_ref.shape
    for k in range(blocks):
        row = lax.rsqrt(1.0 + mine_ref[k : k + 1, :] + other_ref[k : k + 1, :])
        out_ref[k * tb : (k + 1) * tb, :] = jnp.broadcast_to(row, (tb, tb)).T


def run_tiles(base, groups, first_block, list_ref, full_ref, item_ref, conf_ref, w_ref, acc_ref):
    tb = conf_ref.shape[1]
    blocks = full_ref.shape[0] // tb

    def rows(block):
        return pl.ds(pl.multiple_of(block * tb, tb), tb)

    def body(g, _):
        first = base + g * STEP
        entries = []
        for j in range(STEP):
            e = list_ref[first + j]
            block = (e >> SLOT_BITS) & ((1 << BLOCK_BITS) - 1)
            entries.append((e >> (SLOT_BITS + BLOCK_BITS), block, e & ((1 << SLOT_BITS) - 1)))
        for j, (tile, block, slot) in enumerate(entries):
            u = full_ref[rows(jnp.minimum(block, blocks - 1)), :]
            s = lax.dot_general(u, item_ref[slot], (((1,), (1,)), ((), ())), preferred_element_type=F32)
            w_ref[j] = (conf_ref[tile].astype(F32) * (1.0 - s)).astype(BF16)
        for j, (_, block, slot) in enumerate(entries):
            acc_ref[rows(block - first_block), :] += jnp.dot(w_ref[j], item_ref[slot], preferred_element_type=F32)
        return 0

    lax.fori_loop(0, groups, body, 0)


def fill(item_ref, slot_refs, places):
    tb = item_ref.shape[1]
    for s, ref in zip(places, slot_refs):
        per = ref.shape[0] // tb
        for j in range(per):
            item_ref[s * per + j] = ref[j * tb : (j + 1) * tb, :]


def early(places, count_ref, list_ref, mine_ref, other_ref, conf_ref, *refs):
    slot_refs = refs[: len(places)]
    full_ref, acc_ref, item_ref, w_ref = refs[len(places) :]
    half = mine_ref.shape[1]
    here = pl.multiple_of(count_ref[4] * half, half)
    there = pl.multiple_of((1 - count_ref[4]) * half, half)
    full_ref[:, pl.ds(here, half)] = mine_ref[...]
    full_ref[:, pl.ds(there, half)] = other_ref[...]
    fill(item_ref, slot_refs, places)
    acc_ref[...] = jnp.zeros_like(acc_ref)
    run_tiles(0, count_ref[0], 0, list_ref, full_ref, item_ref, conf_ref, w_ref, acc_ref)


def finish(keep_ref, send_ref, acc_ref, scale_ref, fiber, first):
    rows, half = keep_ref.shape
    here = pl.multiple_of(fiber * half, half)
    there = pl.multiple_of((1 - fiber) * half, half)
    scale = scale_ref[first : first + rows, :]
    send_ref[...] = (acc_ref[:rows, pl.ds(there, half)] * scale).astype(BF16)
    keep_ref[...] = acc_ref[:rows, pl.ds(here, half)] * scale


def middle(places, count_ref, list_ref, full_ref, conf_ref, _, *refs):
    slot_refs = refs[: len(places)]
    acc_ref, item_ref, w_ref = refs[len(places) :]
    base = list_ref.shape[0] // 4
    fill(item_ref, slot_refs, places)
    run_tiles(base, count_ref[1], 0, list_ref, full_ref, item_ref, conf_ref, w_ref, acc_ref)


def late(places, count_ref, list_ref, full_ref, scale_ref, conf_ref, _, *refs):
    slot_refs = refs[: len(places)]
    keep_ref, send_ref, acc_ref, item_ref, w_ref = refs[len(places) :]
    base = list_ref.shape[0] // 4
    fill(item_ref, slot_refs, places)
    run_tiles(2 * base, count_ref[2], 0, list_ref, full_ref, item_ref, conf_ref, w_ref, acc_ref)
    finish(keep_ref, send_ref, acc_ref, scale_ref, count_ref[4], 0)


def second(places, count_ref, list_ref, full_ref, scale_ref, conf_ref, _, *refs):
    slot_refs = refs[: len(places)]
    keep_ref, send_ref, acc_ref, item_ref, w_ref = refs[len(places) :]
    rows = keep_ref.shape[0]
    base = list_ref.shape[0] // 4
    fill(item_ref, slot_refs, places)
    acc_ref[...] = jnp.zeros_like(acc_ref)
    block = rows // conf_ref.shape[1]
    run_tiles(3 * base, count_ref[3], block, list_ref, full_ref, item_ref, conf_ref, w_ref, acc_ref)
    finish(keep_ref, send_ref, acc_ref, scale_ref, count_ref[4], rows)


def gather_items(items, n_blk):
    def swap(x, bits):
        return lax.ppermute(x, "blk", [(i, i ^ bits) for i in range(n_blk)])

    got = {0: items, 2: swap(items, 2)}
    for d in range(4, n_blk, 4):
        low = d & -d
        got[d] = swap(items if d == low else got[d ^ low], d if d == low else low)
    for d in range(4, n_blk, 4):
        got[d | 2] = swap(got[d], 2)
    for d in range(0, n_blk, 2):
        got[d | 1] = swap(got[d], 1)
    return [got[d] for d in range(n_blk)]


def shards(users, items, tile_users, tile_items, confidence):
    n_fiber, n_blk = lax.axis_size("fiber"), lax.axis_size("blk")
    tb = confidence.shape[-1]
    rows, half = users.shape
    blocks = rows // tb
    per = items.shape[0] // tb
    user_list = tile_users.reshape(-1)
    item_list = tile_items.reshape(-1)
    conf = confidence.reshape(-1, tb, tb)
    tiles = conf.shape[0]
    swap_fiber = [(i, n_fiber - 1 - i) for i in range(n_fiber)]
    other = lax.ppermute(users, "fiber", swap_fiber)
    slots = gather_items(items, n_blk)
    places = ([], [], [])
    for d in range(n_blk):
        chip = d >> 1
        places[0 if chip & (chip - 1) == 0 else 2 if chip == n_blk // 2 - 1 else 1].append(d)
    hbm = [pltpu.with_memory_space_constraint(x, pltpu.HBM) for x in (user_list, item_list, conf, users, items)]
    sums, conf_v, mine, slots[0], order, count = pl.pallas_call(
        functools.partial(prepare, n_blk, per, places[1][0]),
        out_shape=(
            jax.ShapeDtypeStruct((blocks, tb), F32),
            jax.ShapeDtypeStruct(conf.shape, BF16),
            jax.ShapeDtypeStruct(users.shape, BF16),
            jax.ShapeDtypeStruct(items.shape, BF16),
            jax.ShapeDtypeStruct((4 * (tiles + STEP),), I32),
            jax.ShapeDtypeStruct((5,), I32),
        ),
        in_specs=[HBM] * 5,
        out_specs=(VM, VM, VM, VM, SM, SM),
        scratch_shapes=[
            pltpu.SMEM((tiles,), I32),
            pltpu.SMEM((tiles,), I32),
            pltpu.SMEM((n_blk * per,), I32),
            pltpu.SMEM((4,), I32),
            pltpu.VMEM((blocks, tb, tb), F32),
            pltpu.SemaphoreType.DMA((8 + 4,)),
        ],
        compiler_params=params(4),
        cost_estimate=pl.CostEstimate(flops=0, bytes_accessed=conf.size * 4, transcendentals=0),
        name="prepare",
    )(*hbm)
    sums_other = lax.ppermute(sums, "fiber", swap_fiber)
    scale = pl.pallas_call(
        scales,
        out_shape=jax.ShapeDtypeStruct((rows, half), F32),
        in_specs=[VM, VM],
        out_specs=VM,
        compiler_params=params(2),
        name="scales",
    )(sums, sums_other)
    scratch = [pltpu.VMEM((n_blk * per, tb, 2 * half), BF16), pltpu.VMEM((STEP, tb, tb), BF16)]
    acc_shape = jax.ShapeDtypeStruct((rows // 2 + tb, 2 * half), F32)
    half_shapes = (jax.ShapeDtypeStruct((rows // 2, half), F32), jax.ShapeDtypeStruct((rows // 2, half), BF16))
    scalars = (count, order)
    full, acc = pl.pallas_call(
        functools.partial(early, places[0]),
        out_shape=(jax.ShapeDtypeStruct((rows, 2 * half), BF16), acc_shape),
        in_specs=[SM] * 2 + [VM] * (3 + len(places[0])),
        out_specs=(VM, VM),
        scratch_shapes=scratch,
        compiler_params=params(TILE_MIB),
        cost_estimate=pl.CostEstimate(flops=tiles * tb * tb * half * 8, bytes_accessed=0, transcendentals=0),
        name="early",
    )(*scalars, mine, other, conf_v, *[slots[d] for d in places[0]])
    acc = pl.pallas_call(
        functools.partial(middle, places[1]),
        out_shape=acc_shape,
        in_specs=[SM] * 2 + [VM] * (3 + len(places[1])),
        out_specs=VM,
        scratch_shapes=scratch,
        input_output_aliases={4: 0},
        compiler_params=params(TILE_MIB),
        cost_estimate=pl.CostEstimate(flops=tiles * tb * tb * half * 4, bytes_accessed=0, transcendentals=0),
        name="middle",
    )(*scalars, full, conf_v, acc, *[slots[d] for d in places[1]])
    keep, send, _ = pl.pallas_call(
        functools.partial(late, places[2]),
        out_shape=(*half_shapes, acc_shape),
        in_specs=[SM] * 2 + [VM] * (4 + len(places[2])),
        out_specs=(VM, VM, VM),
        scratch_shapes=scratch,
        input_output_aliases={5: 2},
        compiler_params=params(TILE_MIB),
        cost_estimate=pl.CostEstimate(flops=tiles * tb * tb * half * 8, bytes_accessed=0, transcendentals=0),
        name="late",
    )(*scalars, full, scale, conf_v, acc, *[slots[d] for d in places[2]])
    arrived = lax.ppermute(send, "fiber", swap_fiber)
    keep2, send2 = pl.pallas_call(
        functools.partial(second, range(n_blk)),
        out_shape=half_shapes,
        in_specs=[SM] * 2 + [VM] * (4 + n_blk),
        out_specs=(VM, VM),
        scratch_shapes=[pltpu.VMEM(acc_shape.shape, F32)] + scratch,
        compiler_params=params(TILE_MIB),
        cost_estimate=pl.CostEstimate(flops=tiles * tb * tb * half * 8, bytes_accessed=0, transcendentals=0),
        name="second",
    )(*scalars, full, scale, conf_v, keep, *slots)
    arrived2 = lax.ppermute(send2, "fiber", swap_fiber)
    return jnp.concatenate([(keep + arrived.astype(F32)).astype(BF16), (keep2 + arrived2.astype(F32)).astype(BF16)])


def solution(mesh):
    in_specs = (
        P("blk", "fiber"),
        P("blk", None),
        P("blk", "fiber", None),
        P("blk", "fiber", None),
        P("blk", "fiber", None, None, None),
    )
    return jax.shard_map(shards, mesh=mesh, in_specs=in_specs, out_specs=P("blk", "fiber"), check_vma=False)
```

time: 57.2 us -> 51.7 us (0.904)
  waiting for transfers between devices: 24.1 us -> 17.3 us
  starting transfers between devices: 13.9 us -> 18.7 us
  local copies, waits for them, and re-layouts: 4.79 us -> 0.01 us
  Pallas kernels: 13.2 us -> 14.5 us
    ppermute x1, waiting for transfers between devices: 12.9 us -> 1.27 us  [shards(): arrived = lax.ppermute(send, 'fiber', swap_fiber)]
    ppermute x0 -> x1, waiting for transfers between devices: none -> 6 us  [shards(): arrived2 = lax.ppermute(send2, 'fiber', swap_fiber)]
    unnamed x12 -> x2, local copies, waits for them, and re-layouts: 4.79 us -> 0.01 us
    pallas_call x3 -> x4, Pallas kernels: 6.71 us -> 11 us  [the longest x1 3.91 us: shards(): pl.pallas_call(functools.partial(second, range(n_blk)), out_shape=half_sh...]
    pallas_call x1, Pallas kernels: 6.12 us -> 3.2 us  [shards(): pl.pallas_call(functools.partial(early, places[0]), out_shape=(jax.ShapeD...]
    ppermute x15, starting transfers between devices: 10.4 us -> 12.2 us  [swap(): return lax.ppermute(x, 'blk', [(i, i ^ bits) for i in range(n_blk)])]
    ppermute x15, waiting for transfers between devices: 7.61 us -> 5.83 us  [swap(): return lax.ppermute(x, 'blk', [(i, i ^ bits) for i in range(n_blk)])]
    ppermute x1, starting transfers between devices: 1.49 us -> 2.97 us  [shards(): other = lax.ppermute(users, 'fiber', swap_fiber)]
  transfers between devices with their start and end apart: 18 -> 19, of which waited for: 7 -> 7; matrix products, arithmetic and copies ran while one was open for 0% -> 0% of each run, Pallas kernels for 19% -> 25%
where the time goes in v2:
time: 51.7 us; the launch traced here: 51.5 us
  starting transfers between devices  18.7 us (36%)
  waiting for transfers between devices  17.3 us (33%)
  Pallas kernels  14.5 us (28%)
  other arithmetic  0.94 us (2%)
    ppermute x15, starting transfers between devices, swap(): return lax.ppermute(x, 'blk', [(i, i ^ bits) for i in range(n_blk)])  12.2 us
    ppermute x1, waiting for transfers between devices, shards(): arrived2 = lax.ppermute(send2, 'fiber', swap_fiber)  6 us
    ppermute x15, waiting for transfers between devices, swap(): return lax.ppermute(x, 'blk', [(i, i ^ bits) for i in range(n_blk)])  5.83 us
    ppermute x1, waiting for transfers between devices, shards(): sums_other = lax.ppermute(sums, 'fiber', swap_fiber)  4.17 us
    pallas_call x1, Pallas kernels, shards(): pl.pallas_call(functools.partial(second, range(n_blk)), out_shape=half_sh...  3.91 us
    pallas_call x1, Pallas kernels, shards(): pl.pallas_call(functools.partial(prepare, n_blk, per, places[1][0]), out_...  3.41 us
    pallas_call x1, Pallas kernels, shards(): pl.pallas_call(functools.partial(early, places[0]), out_shape=(jax.ShapeD...  3.2 us
    ppermute x1, starting transfers between devices, shards(): other = lax.ppermute(users, 'fiber', swap_fiber)  2.97 us
  transfers between devices with their start and end apart: 19, of which 7 were waited for; matrix products, arithmetic and copies ran while one was open for 0% of the time, Pallas kernels for 25%

profile of v2, /device:TPU:0, one launch (start us, length us, event | category | flops | bytes accessed | tf_op | source)
XLA Modules:
  0.0 51.5 jit_solution(11433295401807036086)
XLA Ops:
  0.0 3.0 %collective-permute-start = (bf16[2048,128]{1,0:T(8,128)(2,1)}, bf16[2048,128]{1,0:T(8,128)(2,1)S(1)}, u32[]{:S(2)}, u32[]{:S(2)}) collective-permute-start(bf16[2048,128]{1,0:T(8,128)(2,1)} %mine_hbm.1), channel_id=1, source_target_pairs={{0,16},{16,0},{1,17},{17,1},{2,18},{18,2},{3,19},{19,3},{4,20},{20... | collective-permute-start | bytes 1572872 | tf_op jit(solution)/shard_map/ppermute | solution.py:210
  3.0 1.5 %collective-permute-start.2 = (bf16[256,256]{1,0:T(8,128)(2,1)}, bf16[256,256]{1,0:T(8,128)(2,1)S(1)}, u32[]{:S(2)}, u32[]{:S(2)}) collective-permute-start(bf16[256,256]{1,0:T(8,128)(2,1)} %own_hbm.1), channel_id=1, source_target_pairs={{0,2},{1,3},{2,0},{3,1},{4,6},{5,7},{6,4},{7,5},{8,10},{9,11},{10,... | collective-permute-start | bytes 393224 | tf_op jit(solution)/shard_map/ppermute | solution.py:186
  4.5 2.6 %collective-permute-start.6 = (bf16[256,256]{1,0:T(8,128)(2,1)}, bf16[256,256]{1,0:T(8,128)(2,1)S(1)}, u32[]{:S(2)}, u32[]{:S(2)}) collective-permute-start(bf16[256,256]{1,0:T(8,128)(2,1)} %own_hbm.1), channel_id=1, source_target_pairs={{0,8},{1,9},{2,10},{3,11},{4,12},{5,13},{6,14},{7,15},{8,0},{9,1},... | collective-permute-start | bytes 393224 | tf_op jit(solution)/shard_map/ppermute | solution.py:186
  7.1 0.0 collective-permute-start.1
  7.1 0.0 copy-start
  7.1 3.4 %prepare.1 = (f32[16,128]{1,0:T(8,128)S(1)}, bf16[128,128,128]{2,1,0:T(8,128)(2,1)S(1)}, bf16[2048,128]{1,0:T(8,128)(2,1)S(1)}, bf16[256,256]{1,0:T(8,128)(2,1)S(1)}, s32[576]{0:T(1024)S(1)}, /*index=5*/s32[5]{0:T(128)S(1)}) custom-call(s32[128]{0:T(128)} %bitcast.4, s32[128]{0:T(128)} %bitcast.5, bf16[128,128,128]{2,1,0:T(8,128)(2,1)} %bitcast.3, ...), custom_call_target="tpu_custom_call" | custom-call | bytes 8388608 | tf_op jit(solution)/shard_map/prepare/pallas_call | solution.py:217
  10.5 0.6 %collective-permute-start.8 = (f32[16,128]{1,0:T(8,128)S(1)}, f32[16,128]{1,0:T(8,128)S(1)}, u32[]{:S(2)}, u32[]{:S(2)}) collective-permute-start(f32[16,128]{1,0:T(8,128)S(1)} %get-tuple-element.23.mine_ref), channel_id=1, source_target_pairs={{0,16},{16,0},{1,17},{17,1},{2,18},{18,2},{3,19},{19,3},{4,20},{20... | collective-permute-start | bytes 24584 | tf_op jit(solution)/shard_map/ppermute | solution.py:241
  11.1 4.2 %collective-permute-done.8.other_ref = f32[16,128]{1,0:T(8,128)S(1)} collective-permute-done((f32[16,128]{1,0:T(8,128)S(1)}, f32[16,128]{1,0:T(8,128)S(1)}, u32[]{:S(2)}, u32[]{:S(2)}) %collective-permute-start.8) | collective-permute-done | bytes 8224 | tf_op jit(solution)/shard_map/ppermute | solution.py:241
  15.3 0.0 copy-done
  15.3 1.8 %collective-permute-start.4 = (bf16[256,256]{1,0:T(8,128)(2,1)S(1)}, bf16[256,256]{1,0:T(8,128)(2,1)S(1)}, u32[]{:S(2)}, u32[]{:S(2)}) collective-permute-start(bf16[256,256]{1,0:T(8,128)(2,1)S(1)} %copy-done), channel_id=1, source_target_pairs={{0,4},{1,5},{2,6},{3,7},{4,0},{5,1},{6,2},{7,3},{8,12},{9,13},{10,... | collective-permute-start | bytes 393224 | tf_op jit(solution)/shard_map/ppermute | solution.py:186
  17.1 0.0 collective-permute-done.2.refs_2_
  17.1 0.0 collective-permute-start.3
  17.1 0.0 collective-permute-done.6.refs_6_.refs_8_
  17.1 0.3 collective-permute-start.13
  17.4 0.0 collective-permute-done.1.refs_1_
  17.4 1.8 %collective-permute-start.11 = (bf16[256,256]{1,0:T(8,128)(2,1)S(1)}, bf16[256,256]{1,0:T(8,128)(2,1)S(1)}, u32[]{:S(2)}, u32[]{:S(2)}) collective-permute-start(bf16[256,256]{1,0:T(8,128)(2,1)S(1)} %collective-permute-done.6.refs_6_.refs_8_), channel_id=1, source_target_pairs={{0,2},{1,3},{2,0},{3,1},{4,6},{5,7},{6,4},{7,5},{8,10},{9,11},{10,... | collective-permute-start | bytes 393224 | tf_op jit(solution)/shard_map/ppermute | solution.py:186
  19.2 1.7 %collective-permute-done.4.refs_4_ = bf16[256,256]{1,0:T(8,128)(2,1)S(1)} collective-permute-done((bf16[256,256]{1,0:T(8,128)(2,1)S(1)}, bf16[256,256]{1,0:T(8,128)(2,1)S(1)}, u32[]{:S(2)}, u32[]{:S(2)}) %collective-permute-start.4) | collective-permute-done | bytes 131104 | tf_op jit(solution)/shard_map/ppermute | solution.py:186
  20.8 0.0 collective-permute-start.7
  20.8 0.0 collective-permute-done.3.refs_3_
  20.8 1.7 %collective-permute-start.9 = (bf16[256,256]{1,0:T(8,128)(2,1)S(1)}, bf16[256,256]{1,0:T(8,128)(2,1)S(1)}, u32[]{:S(2)}, u32[]{:S(2)}) collective-permute-start(bf16[256,256]{1,0:T(8,128)(2,1)S(1)} %collective-permute-done.4.refs_4_), channel_id=1, source_target_pairs={{0,2},{1,3},{2,0},{3,1},{4,6},{5,7},{6,4},{7,5},{8,10},{9,11},{10,... | collective-permute-start | bytes 393224 | tf_op jit(solution)/shard_map/ppermute | solution.py:186
  22.5 0.5 %collective-permute-done.13.refs_4_.refs_12_ = bf16[256,256]{1,0:T(8,128)(2,1)S(1)} collective-permute-done((bf16[256,256]{1,0:T(8,128)(2,1)S(1)}, bf16[256,256]{1,0:T(8,128)(2,1)S(1)}, u32[]{:S(2)}, u32[]{:S(2)}) %collective-permute-start.13) | collective-permute-done | bytes 131104 | tf_op jit(solution)/shard_map/ppermute | solution.py:186
  23.1 0.0 collective-permute-start.5
  23.1 0.0 collective-permute-done.11.refs_2_.refs_10_
  23.1 1.7 %collective-permute-start.15 = (bf16[256,256]{1,0:T(8,128)(2,1)S(1)}, bf16[256,256]{1,0:T(8,128)(2,1)S(1)}, u32[]{:S(2)}, u32[]{:S(2)}) collective-permute-start(bf16[256,256]{1,0:T(8,128)(2,1)S(1)} %collective-permute-done.13.refs_4_.refs_12_), channel_id=1, source_target_pairs={{0,2},{1,3},{2,0},{3,1},{4,6},{5,7},{6,4},{7,5},{8,10},{9,11},{10,... | collective-permute-start | bytes 393224 | tf_op jit(solution)/shard_map/ppermute | solution.py:186
  24.8 0.3 scales.1.scale_ref
  25.2 0.0 collective-permute-done.7.refs_7_.refs_9_
  25.2 0.3 collective-permute-start.14
  25.5 1.7 %collective-permute-done.9.refs_0_.refs_6_ = bf16[256,256]{1,0:T(8,128)(2,1)S(1)} collective-permute-done((bf16[256,256]{1,0:T(8,128)(2,1)S(1)}, bf16[256,256]{1,0:T(8,128)(2,1)S(1)}, u32[]{:S(2)}, u32[]{:S(2)}) %collective-permute-start.9) | collective-permute-done | bytes 131104 | tf_op jit(solution)/shard_map/ppermute | solution.py:186
  27.2 0.0 collective-permute-start.12
  27.2 0.0 collective-permute-done.5.refs_5_
  27.2 0.5 collective-permute-start.10
  27.7 1.8 %collective-permute-done.15.refs_0_.refs_14_ = bf16[256,256]{1,0:T(8,128)(2,1)S(1)} collective-permute-done((bf16[256,256]{1,0:T(8,128)(2,1)S(1)}, bf16[256,256]{1,0:T(8,128)(2,1)S(1)}, u32[]{:S(2)}, u32[]{:S(2)}) %collective-permute-start.15) | collective-permute-done | bytes 131104 | tf_op jit(solution)/shard_map/ppermute | solution.py:186
  29.6 0.0 collective-permute-start.16
  29.6 0.0 collective-permute-done.other_ref
  29.6 3.2 %early.1 = (bf16[2048,256]{1,0:T(8,128)(2,1)S(1)}, f32[1152,256]{1,0:T(8,128)S(1)}) custom-call(s32[5]{0:T(128)S(1)} %get-tuple-element.17.count_ref, s32[576]{0:T(1024)S(1)} %get-tuple-element.18.list_ref, bf16[2048,128]{1,0:T(8,128)(2,1)S(1)} %get-tuple-element.19.mine_ref, bf16[2048,128]{1,0:T(8,128)(2,1)S(1)} %collective-permute-done.other_ref, ...), custom_call_target="tpu_custom_call" | custom-call | flops 2147483648 | tf_op jit(solution)/shard_map/early/pallas_call | solution.py:254
  32.8 0.0 collective-permute-done.14.refs_5_.refs_13_
  32.8 0.0 collective-permute-done.12.refs_3_.refs_11_
  32.8 0.0 collective-permute-done.10.refs_1_.refs_7_
  32.8 2.2 %middle.1._ = f32[1152,256]{1,0:T(8,128)S(1)} custom-call(s32[5]{0:T(128)S(1)} %get-tuple-element.17.count_ref, s32[576]{0:T(1024)S(1)} %get-tuple-element.18.list_ref, bf16[2048,256]{1,0:T(8,128)(2,1)S(1)} %get-tuple-element.22.full_ref, bf16[128,128,128]{2,1,0:T(8,128)(2,1)S(1)} %get-tuple-element.20.conf_ref, ...), custom_call_target="tpu_custom_call", output_to_operand_aliasing={{}: (4, {})} | custom-call | flops 1073741824 | tf_op jit(solution)/shard_map/middle/pallas_call | solution.py:264
  35.0 0.0 collective-permute-done.16.refs_1_.refs_15_
  35.0 1.5 %late.1 = (f32[1024,128]{1,0:T(8,128)S(1)}, bf16[1024,128]{1,0:T(8,128)(2,1)S(1)}, f32[1152,256]{1,0:T(8,128)S(1)}) custom-call(s32[5]{0:T(128)S(1)} %get-tuple-element.17.count_ref, s32[576]{0:T(1024)S(1)} %get-tuple-element.18.list_ref, bf16[2048,256]{1,0:T(8,128)(2,1)S(1)} %get-tuple-element.22.full_ref, ...), custom_call_target="tpu_custom_call", output_to_operand_aliasing={{2}: (5, {})} | custom-call | flops 2147483648 | tf_op jit(solution)/shard_map/late/pallas_call | solution.py:275
  36.5 1.7 %collective-permute-start.17 = (bf16[1024,128]{1,0:T(8,128)(2,1)S(1)}, bf16[1024,128]{1,0:T(8,128)(2,1)S(1)}, u32[]{:S(2)}, u32[]{:S(2)}) collective-permute-start(bf16[1024,128]{1,0:T(8,128)(2,1)S(1)} %get-tuple-element.26), channel_id=1, source_target_pairs={{0,16},{16,0},{1,17},{17,1},{2,18},{18,2},{3,19},{19,3},{4,20},{20... | collective-permute-start | bytes 786440 | tf_op jit(solution)/shard_map/ppermute | solution.py:286
  38.2 3.9 %second.1 = (f32[1024,128]{1,0:T(8,128)S(1)}, bf16[1024,128]{1,0:T(8,128)(2,1)S(1)}) custom-call(s32[5]{0:T(128)S(1)} %get-tuple-element.17.count_ref, s32[576]{0:T(1024)S(1)} %get-tuple-element.18.list_ref, bf16[2048,256]{1,0:T(8,128)(2,1)S(1)} %get-tuple-element.22.full_ref, f32[2048,128]{1,0:T(8,128)S(1)} %scales.1.scale_ref, ...), custom_call_target="tpu_custom_call" | custom-call | flops 2147483648 | tf_op jit(solution)/shard_map/second/pallas_call | solution.py:287
  42.2 1.2 %collective-permute-start.18 = (bf16[1024,128]{1,0:T(8,128)(2,1)S(1)}, bf16[1024,128]{1,0:T(8,128)(2,1)S(1)}, u32[]{:S(2)}, u32[]{:S(2)}) collective-permute-start(bf16[1024,128]{1,0:T(8,128)(2,1)S(1)} %get-tuple-element.28), channel_id=1, source_target_pairs={{0,16},{16,0},{1,17},{17,1},{2,18},{18,2},{3,19},{19,3},{4,20},{20... | collective-permute-start | bytes 786440 | tf_op jit(solution)/shard_map/ppermute | solution.py:297
  43.3 1.3 %collective-permute-done.17 = bf16[1024,128]{1,0:T(8,128)(2,1)S(1)} collective-permute-done((bf16[1024,128]{1,0:T(8,128)(2,1)S(1)}, bf16[1024,128]{1,0:T(8,128)(2,1)S(1)}, u32[]{:S(2)}, u32[]{:S(2)}) %collective-permute-start.17) | collective-permute-done | bytes 262176 | tf_op jit(solution)/shard_map/ppermute | solution.py:286
  44.6 0.1 add_convert_fusion.1
  44.6 6.0 %collective-permute-done.18 = bf16[1024,128]{1,0:T(8,128)(2,1)S(1)} collective-permute-done((bf16[1024,128]{1,0:T(8,128)(2,1)S(1)}, bf16[1024,128]{1,0:T(8,128)(2,1)S(1)}, u32[]{:S(2)}, u32[]{:S(2)}) %collective-permute-start.18) | collective-permute-done | bytes 262176 | tf_op jit(solution)/shard_map/ppermute | solution.py:297
  50.6 0.1 add_convert_fusion
  50.7 0.8 %pad_maximum_fusion = bf16[2048,128]{1,0:T(8,128)(2,1)} fusion(bf16[1024,128]{1,0:T(8,128)(2,1)S(1)} %add_convert_fusion, bf16[1024,128]{1,0:T(8,128)(2,1)S(1)} %add_convert_fusion.1), kind=kLoop, calls=%fused_computation | loop fusion | flops 1048576 | bytes 1048576 | tf_op jit(solution)/shard_map/concatenate | solution.py:298
Async XLA Ops:
  0.0 29.6 %collective-permute-start = (bf16[2048,128]{1,0:T(8,128)(2,1)}, bf16[2048,128]{1,0:T(8,128)(2,1)S(1)}, u32[]{:S(2)}, u32[]{:S(2)}) collective-permute-start(bf16[2048,128]{1,0:T(8,128)(2,1)} %mine_hbm.1), channel_id=1, source_target_pairs={{0,16},{16,0},{1,17},{17,1},{2,18},{18,2},{3,19},{19,3},{4,20},{20... | collective-permute-start | bytes 1572872 | tf_op jit(solution)/shard_map/ppermute | solution.py:210
  3.0 14.1 %collective-permute-start.2 = (bf16[256,256]{1,0:T(8,128)(2,1)}, bf16[256,256]{1,0:T(8,128)(2,1)S(1)}, u32[]{:S(2)}, u32[]{:S(2)}) collective-permute-start(bf16[256,256]{1,0:T(8,128)(2,1)} %own_hbm.1), channel_id=1, source_target_pairs={{0,2},{1,3},{2,0},{3,1},{4,6},{5,7},{6,4},{7,5},{8,10},{9,11},{10,... | collective-permute-start | bytes 393224 | tf_op jit(solution)/shard_map/ppermute | solution.py:186
  4.5 12.6 %collective-permute-start.6 = (bf16[256,256]{1,0:T(8,128)(2,1)}, bf16[256,256]{1,0:T(8,128)(2,1)S(1)}, u32[]{:S(2)}, u32[]{:S(2)}) collective-permute-start(bf16[256,256]{1,0:T(8,128)(2,1)} %own_hbm.1), channel_id=1, source_target_pairs={{0,8},{1,9},{2,10},{3,11},{4,12},{5,13},{6,14},{7,15},{8,0},{9,1},... | collective-permute-start | bytes 393224 | tf_op jit(solution)/shard_map/ppermute | solution.py:186
  7.1 10.3 %collective-permute-start.1 = (bf16[256,256]{1,0:T(8,128)(2,1)}, bf16[256,256]{1,0:T(8,128)(2,1)S(1)}, u32[]{:S(2)}, u32[]{:S(2)}) collective-permute-start(bf16[256,256]{1,0:T(8,128)(2,1)} %own_hbm.1), channel_id=1, source_target_pairs={{0,1},{1,0},{2,3},{3,2},{4,5},{5,4},{6,7},{7,6},{8,9},{9,8},{10,11... | collective-permute-start | bytes 393224 | tf_op jit(solution)/shard_map/ppermute | solution.py:186
  7.1 8.2 %copy-start = (bf16[256,256]{1,0:T(8,128)(2,1)S(1)}, bf16[256,256]{1,0:T(8,128)(2,1)}, u32[]{:S(2)}) copy-start(bf16[256,256]{1,0:T(8,128)(2,1)} %own_hbm.1) | copy-start | bytes 393220
  10.5 4.8 %collective-permute-start.8 = (f32[16,128]{1,0:T(8,128)S(1)}, f32[16,128]{1,0:T(8,128)S(1)}, u32[]{:S(2)}, u32[]{:S(2)}) collective-permute-start(f32[16,128]{1,0:T(8,128)S(1)} %get-tuple-element.23.mine_ref), channel_id=1, source_target_pairs={{0,16},{16,0},{1,17},{17,1},{2,18},{18,2},{3,19},{19,3},{4,20},{20... | collective-permute-start | bytes 24584 | tf_op jit(solution)/shard_map/ppermute | solution.py:241
  15.3 5.6 %collective-permute-start.4 = (bf16[256,256]{1,0:T(8,128)(2,1)S(1)}, bf16[256,256]{1,0:T(8,128)(2,1)S(1)}, u32[]{:S(2)}, u32[]{:S(2)}) collective-permute-start(bf16[256,256]{1,0:T(8,128)(2,1)S(1)} %copy-done), channel_id=1, source_target_pairs={{0,4},{1,5},{2,6},{3,7},{4,0},{5,1},{6,2},{7,3},{8,12},{9,13},{10,... | collective-permute-start | bytes 393224 | tf_op jit(solution)/shard_map/ppermute | solution.py:186
  17.1 3.7 %collective-permute-start.3 = (bf16[256,256]{1,0:T(8,128)(2,1)S(1)}, bf16[256,256]{1,0:T(8,128)(2,1)S(1)}, u32[]{:S(2)}, u32[]{:S(2)}) collective-permute-start(bf16[256,256]{1,0:T(8,128)(2,1)S(1)} %collective-permute-done.2.refs_2_), channel_id=1, source_target_pairs={{0,1},{1,0},{2,3},{3,2},{4,5},{5,4},{6,7},{7,6},{8,9},{9,8},{10,11... | collective-permute-start | bytes 393224 | tf_op jit(solution)/shard_map/ppermute | solution.py:186
  17.1 5.9 %collective-permute-start.13 = (bf16[256,256]{1,0:T(8,128)(2,1)S(1)}, bf16[256,256]{1,0:T(8,128)(2,1)S(1)}, u32[]{:S(2)}, u32[]{:S(2)}) collective-permute-start(bf16[256,256]{1,0:T(8,128)(2,1)S(1)} %collective-permute-done.6.refs_6_.refs_8_), channel_id=1, source_target_pairs={{0,4},{1,5},{2,6},{3,7},{4,0},{5,1},{6,2},{7,3},{8,12},{9,13},{10,... | collective-permute-start | bytes 393224 | tf_op jit(solution)/shard_map/ppermute | solution.py:186
  17.4 5.7 %collective-permute-start.11 = (bf16[256,256]{1,0:T(8,128)(2,1)S(1)}, bf16[256,256]{1,0:T(8,128)(2,1)S(1)}, u32[]{:S(2)}, u32[]{:S(2)}) collective-permute-start(bf16[256,256]{1,0:T(8,128)(2,1)S(1)} %collective-permute-done.6.refs_6_.refs_8_), channel_id=1, source_target_pairs={{0,2},{1,3},{2,0},{3,1},{4,6},{5,7},{6,4},{7,5},{8,10},{9,11},{10,... | collective-permute-start | bytes 393224 | tf_op jit(solution)/shard_map/ppermute | solution.py:186
  20.8 4.4 %collective-permute-start.7 = (bf16[256,256]{1,0:T(8,128)(2,1)S(1)}, bf16[256,256]{1,0:T(8,128)(2,1)S(1)}, u32[]{:S(2)}, u32[]{:S(2)}) collective-permute-start(bf16[256,256]{1,0:T(8,128)(2,1)S(1)} %collective-permute-done.6.refs_6_.refs_8_), channel_id=1, source_target_pairs={{0,1},{1,0},{2,3},{3,2},{4,5},{5,4},{6,7},{7,6},{8,9},{9,8},{10,11... | collective-permute-start | bytes 393224 | tf_op jit(solution)/shard_map/ppermute | solution.py:186
  20.8 6.4 %collective-permute-start.9 = (bf16[256,256]{1,0:T(8,128)(2,1)S(1)}, bf16[256,256]{1,0:T(8,128)(2,1)S(1)}, u32[]{:S(2)}, u32[]{:S(2)}) collective-permute-start(bf16[256,256]{1,0:T(8,128)(2,1)S(1)} %collective-permute-done.4.refs_4_), channel_id=1, source_target_pairs={{0,2},{1,3},{2,0},{3,1},{4,6},{5,7},{6,4},{7,5},{8,10},{9,11},{10,... | collective-permute-start | bytes 393224 | tf_op jit(solution)/shard_map/ppermute | solution.py:186
  23.1 4.2 %collective-permute-start.5 = (bf16[256,256]{1,0:T(8,128)(2,1)S(1)}, bf16[256,256]{1,0:T(8,128)(2,1)S(1)}, u32[]{:S(2)}, u32[]{:S(2)}) collective-permute-start(bf16[256,256]{1,0:T(8,128)(2,1)S(1)} %collective-permute-done.4.refs_4_), channel_id=1, source_target_pairs={{0,1},{1,0},{2,3},{3,2},{4,5},{5,4},{6,7},{7,6},{8,9},{9,8},{10,11... | collective-permute-start | bytes 393224 | tf_op jit(solution)/shard_map/ppermute | solution.py:186
  23.1 6.5 %collective-permute-start.15 = (bf16[256,256]{1,0:T(8,128)(2,1)S(1)}, bf16[256,256]{1,0:T(8,128)(2,1)S(1)}, u32[]{:S(2)}, u32[]{:S(2)}) collective-permute-start(bf16[256,256]{1,0:T(8,128)(2,1)S(1)} %collective-permute-done.13.refs_4_.refs_12_), channel_id=1, source_target_pairs={{0,2},{1,3},{2,0},{3,1},{4,6},{5,7},{6,4},{7,5},{8,10},{9,11},{10,... | collective-permute-start | bytes 393224 | tf_op jit(solution)/shard_map/ppermute | solution.py:186
  25.2 7.6 %collective-permute-start.14 = (bf16[256,256]{1,0:T(8,128)(2,1)S(1)}, bf16[256,256]{1,0:T(8,128)(2,1)S(1)}, u32[]{:S(2)}, u32[]{:S(2)}) collective-permute-start(bf16[256,256]{1,0:T(8,128)(2,1)S(1)} %collective-permute-done.13.refs_4_.refs_12_), channel_id=1, source_target_pairs={{0,1},{1,0},{2,3},{3,2},{4,5},{5,4},{6,7},{7,6},{8,9},{9,8},{10,11... | collective-permute-start | bytes 393224 | tf_op jit(solution)/shard_map/ppermute | solution.py:186
  27.2 5.6 %collective-permute-start.12 = (bf16[256,256]{1,0:T(8,128)(2,1)S(1)}, bf16[256,256]{1,0:T(8,128)(2,1)S(1)}, u32[]{:S(2)}, u32[]{:S(2)}) collective-permute-start(bf16[256,256]{1,0:T(8,128)(2,1)S(1)} %collective-permute-done.11.refs_2_.refs_10_), channel_id=1, source_target_pairs={{0,1},{1,0},{2,3},{3,2},{4,5},{5,4},{6,7},{7,6},{8,9},{9,8},{10,11... | collective-permute-start | bytes 393224 | tf_op jit(solution)/shard_map/ppermute | solution.py:186
  27.2 5.6 %collective-permute-start.10 = (bf16[256,256]{1,0:T(8,128)(2,1)S(1)}, bf16[256,256]{1,0:T(8,128)(2,1)S(1)}, u32[]{:S(2)}, u32[]{:S(2)}) collective-permute-start(bf16[256,256]{1,0:T(8,128)(2,1)S(1)} %collective-permute-done.9.refs_0_.refs_6_), channel_id=1, source_target_pairs={{0,1},{1,0},{2,3},{3,2},{4,5},{5,4},{6,7},{7,6},{8,9},{9,8},{10,11... | collective-permute-start | bytes 393224 | tf_op jit(solution)/shard_map/ppermute | solution.py:186
  29.6 5.4 %collective-permute-start.16 = (bf16[256,256]{1,0:T(8,128)(2,1)S(1)}, bf16[256,256]{1,0:T(8,128)(2,1)S(1)}, u32[]{:S(2)}, u32[]{:S(2)}) collective-permute-start(bf16[256,256]{1,0:T(8,128)(2,1)S(1)} %collective-permute-done.15.refs_0_.refs_14_), channel_id=1, source_target_pairs={{0,1},{1,0},{2,3},{3,2},{4,5},{5,4},{6,7},{7,6},{8,9},{9,8},{10,11... | collective-permute-start | bytes 393224 | tf_op jit(solution)/shard_map/ppermute | solution.py:186
  36.5 8.1 %collective-permute-start.17 = (bf16[1024,128]{1,0:T(8,128)(2,1)S(1)}, bf16[1024,128]{1,0:T(8,128)(2,1)S(1)}, u32[]{:S(2)}, u32[]{:S(2)}) collective-permute-start(bf16[1024,128]{1,0:T(8,128)(2,1)S(1)} %get-tuple-element.26), channel_id=1, source_target_pairs={{0,16},{16,0},{1,17},{17,1},{2,18},{18,2},{3,19},{19,3},{4,20},{20... | collective-permute-start | bytes 786440 | tf_op jit(solution)/shard_map/ppermute | solution.py:286
  42.2 8.5 %collective-permute-start.18 = (bf16[1024,128]{1,0:T(8,128)(2,1)S(1)}, bf16[1024,128]{1,0:T(8,128)(2,1)S(1)}, u32[]{:S(2)}, u32[]{:S(2)}) collective-permute-start(bf16[1024,128]{1,0:T(8,128)(2,1)S(1)} %get-tuple-element.28), channel_id=1, source_target_pairs={{0,16},{16,0},{1,17},{17,1},{2,18},{18,2},{3,19},{19,3},{4,20},{20... | collective-permute-start | bytes 786440 | tf_op jit(solution)/shard_map/ppermute | solution.py:297

commit v3 on v2

--- a/solution.py
+++ b/solution.py
@@ -179,6 +179,20 @@
     block = rows // conf_ref.shape[1]
     run_tiles(3 * base, count_ref[3], block, list_ref, full_ref, item_ref, conf_ref, w_ref, acc_ref)
     finish(keep_ref, send_ref, acc_ref, scale_ref, count_ref[4], rows)
+
+
+def write(part, keep_ref, came_ref, *refs):
+    out_ref, buf, sems = refs[-3:]
+    rows = keep_ref.shape[0]
+    piece = rows // 2
+    copies = []
+    for i in range(2):
+        at = pl.ds(i * piece, piece)
+        buf[at, :] = (keep_ref[at, :] + came_ref[at, :].astype(F32)).astype(BF16)
+        copies.append(pltpu.make_async_copy(buf.at[at], out_ref.at[pl.ds(part * rows + i * piece, piece)], sems.at[i]))
+        copies[-1].start()
+    for c in copies:
+        c.wait()
 
 
 def gather_items(items, n_blk):
@@ -295,7 +309,18 @@
         name="second",
     )(*scalars, full, scale, conf_v, keep, *slots)
     arrived2 = lax.ppermute(send2, "fiber", swap_fiber)
-    return jnp.concatenate([(keep + arrived.astype(F32)).astype(BF16), (keep2 + arrived2.astype(F32)).astype(BF16)])
+    out = None
+    for i, (kept, came) in enumerate(((keep, arrived), (keep2, arrived2))):
+        out = pl.pallas_call(
+            functools.partial(write, i),
+            out_shape=pltpu.HBM(users.shape, BF16),
+            in_specs=[VM, VM] + [HBM] * i,
+            out_specs=HBM,
+            scratch_shapes=[pltpu.VMEM(came.shape, BF16), pltpu.SemaphoreType.DMA((2,))],
+            input_output_aliases={2: 0} if i else {},
+            compiler_params=params(2),
+        )(kept, came, *([out] if i else []))
+    return out
 
 
 def solution(mesh):

time: 51.7 us -> 51.5 us (level)
  Pallas kernels: 14.5 us -> 16 us
  other arithmetic: 0.94 us -> 0 us
  waiting for transfers between devices: 17.3 us -> 16.6 us
    pallas_call x0 -> x2, Pallas kernels: none -> 1.49 us  [shards(): pl.pallas_call(functools.partial(write, i), out_shape=pltpu.HBM(users.sha...]
    concatenate x1 -> x0, other arithmetic: 0.83 us -> none  [shards(): jnp.concatenate([(keep + arrived.astype(F32)).astype(BF16), (keep2 + arri...]
    ppermute x1, waiting for transfers between devices: 6 us -> 5.31 us  [shards(): arrived2 = lax.ppermute(send2, 'fiber', swap_fiber)]
  transfers between devices with their start and end apart: 19 -> 19, of which waited for: 7 -> 7; matrix products, arithmetic and copies ran while one was open for 0% -> 0% of each run, Pallas kernels for 25% -> 27%
where the time goes in v3:
time: 51.5 us; the launch traced here: 51.4 us
  starting transfers between devices  18.7 us (36%)
  waiting for transfers between devices  16.6 us (32%)
  Pallas kernels  16 us (31%)
    ppermute x15, starting transfers between devices, swap(): return lax.ppermute(x, 'blk', [(i, i ^ bits) for i in range(n_blk)])  12.2 us
    ppermute x15, waiting for transfers between devices, swap(): return lax.ppermute(x, 'blk', [(i, i ^ bits) for i in range(n_blk)])  5.83 us
    ppermute x1, waiting for transfers between devices, shards(): arrived2 = lax.ppermute(send2, 'fiber', swap_fiber)  5.31 us
    ppermute x1, waiting for transfers between devices, shards(): sums_other = lax.ppermute(sums, 'fiber', swap_fiber)  4.17 us
    pallas_call x1, Pallas kernels, shards(): pl.pallas_call(functools.partial(second, range(n_blk)), out_shape=half_sh...  3.91 us
    pallas_call x1, Pallas kernels, shards(): pl.pallas_call(functools.partial(prepare, n_blk, per, places[1][0]), out_...  3.41 us
    pallas_call x1, Pallas kernels, shards(): pl.pallas_call(functools.partial(early, places[0]), out_shape=(jax.ShapeD...  3.2 us
    ppermute x1, starting transfers between devices, shards(): other = lax.ppermute(users, 'fiber', swap_fiber)  2.97 us
  transfers between devices with their start and end apart: 19, of which 7 were waited for; matrix products, arithmetic and copies ran while one was open for 0% of the time, Pallas kernels for 27%

profile of v3, /device:TPU:0, one launch (start us, length us, event | category | flops | bytes accessed | tf_op | source)
XLA Modules:
  0.0 51.4 jit_solution(7166698094277663703)
XLA Ops:
  0.0 3.0 %collective-permute-start = (bf16[2048,128]{1,0:T(8,128)(2,1)}, bf16[2048,128]{1,0:T(8,128)(2,1)S(1)}, u32[]{:S(2)}, u32[]{:S(2)}) collective-permute-start(bf16[2048,128]{1,0:T(8,128)(2,1)} %mine_hbm.1), channel_id=1, source_target_pairs={{0,16},{16,0},{1,17},{17,1},{2,18},{18,2},{3,19},{19,3},{4,20},{20... | collective-permute-start | bytes 1572872 | tf_op jit(solution)/shard_map/ppermute | solution.py:224
  3.0 1.5 %collective-permute-start.2 = (bf16[256,256]{1,0:T(8,128)(2,1)}, bf16[256,256]{1,0:T(8,128)(2,1)S(1)}, u32[]{:S(2)}, u32[]{:S(2)}) collective-permute-start(bf16[256,256]{1,0:T(8,128)(2,1)} %own_hbm.1), channel_id=1, source_target_pairs={{0,2},{1,3},{2,0},{3,1},{4,6},{5,7},{6,4},{7,5},{8,10},{9,11},{10,... | collective-permute-start | bytes 393224 | tf_op jit(solution)/shard_map/ppermute | solution.py:200
  4.5 2.6 %collective-permute-start.6 = (bf16[256,256]{1,0:T(8,128)(2,1)}, bf16[256,256]{1,0:T(8,128)(2,1)S(1)}, u32[]{:S(2)}, u32[]{:S(2)}) collective-permute-start(bf16[256,256]{1,0:T(8,128)(2,1)} %own_hbm.1), channel_id=1, source_target_pairs={{0,8},{1,9},{2,10},{3,11},{4,12},{5,13},{6,14},{7,15},{8,0},{9,1},... | collective-permute-start | bytes 393224 | tf_op jit(solution)/shard_map/ppermute | solution.py:200
  7.1 0.0 collective-permute-start.1
  7.1 0.0 copy-start
  7.1 3.4 %prepare.1 = (f32[16,128]{1,0:T(8,128)S(1)}, bf16[128,128,128]{2,1,0:T(8,128)(2,1)S(1)}, bf16[2048,128]{1,0:T(8,128)(2,1)S(1)}, bf16[256,256]{1,0:T(8,128)(2,1)S(1)}, s32[576]{0:T(1024)S(1)}, /*index=5*/s32[5]{0:T(128)S(1)}) custom-call(s32[128]{0:T(128)} %bitcast.4, s32[128]{0:T(128)} %bitcast.5, bf16[128,128,128]{2,1,0:T(8,128)(2,1)} %bitcast.3, ...), custom_call_target="tpu_custom_call" | custom-call | bytes 8388608 | tf_op jit(solution)/shard_map/prepare/pallas_call | solution.py:231
  10.5 0.6 %collective-permute-start.8 = (f32[16,128]{1,0:T(8,128)S(1)}, f32[16,128]{1,0:T(8,128)S(1)}, u32[]{:S(2)}, u32[]{:S(2)}) collective-permute-start(f32[16,128]{1,0:T(8,128)S(1)} %get-tuple-element.23.mine_ref), channel_id=1, source_target_pairs={{0,16},{16,0},{1,17},{17,1},{2,18},{18,2},{3,19},{19,3},{4,20},{20... | collective-permute-start | bytes 24584 | tf_op jit(solution)/shard_map/ppermute | solution.py:255
  11.1 4.2 %collective-permute-done.8.other_ref = f32[16,128]{1,0:T(8,128)S(1)} collective-permute-done((f32[16,128]{1,0:T(8,128)S(1)}, f32[16,128]{1,0:T(8,128)S(1)}, u32[]{:S(2)}, u32[]{:S(2)}) %collective-permute-start.8) | collective-permute-done | bytes 8224 | tf_op jit(solution)/shard_map/ppermute | solution.py:255
  15.3 0.0 copy-done
  15.3 1.8 %collective-permute-start.4 = (bf16[256,256]{1,0:T(8,128)(2,1)S(1)}, bf16[256,256]{1,0:T(8,128)(2,1)S(1)}, u32[]{:S(2)}, u32[]{:S(2)}) collective-permute-start(bf16[256,256]{1,0:T(8,128)(2,1)S(1)} %copy-done), channel_id=1, source_target_pairs={{0,4},{1,5},{2,6},{3,7},{4,0},{5,1},{6,2},{7,3},{8,12},{9,13},{10,... | collective-permute-start | bytes 393224 | tf_op jit(solution)/shard_map/ppermute | solution.py:200
  17.1 0.0 collective-permute-done.2.refs_2_
  17.1 0.0 collective-permute-start.3
  17.1 0.0 collective-permute-done.6.refs_6_.refs_8_
  17.1 0.3 collective-permute-start.13
  17.4 0.0 collective-permute-done.1.refs_1_
  17.4 1.8 %collective-permute-start.11 = (bf16[256,256]{1,0:T(8,128)(2,1)S(1)}, bf16[256,256]{1,0:T(8,128)(2,1)S(1)}, u32[]{:S(2)}, u32[]{:S(2)}) collective-permute-start(bf16[256,256]{1,0:T(8,128)(2,1)S(1)} %collective-permute-done.6.refs_6_.refs_8_), channel_id=1, source_target_pairs={{0,2},{1,3},{2,0},{3,1},{4,6},{5,7},{6,4},{7,5},{8,10},{9,11},{10,... | collective-permute-start | bytes 393224 | tf_op jit(solution)/shard_map/ppermute | solution.py:200
  19.2 1.7 %collective-permute-done.4.refs_4_ = bf16[256,256]{1,0:T(8,128)(2,1)S(1)} collective-permute-done((bf16[256,256]{1,0:T(8,128)(2,1)S(1)}, bf16[256,256]{1,0:T(8,128)(2,1)S(1)}, u32[]{:S(2)}, u32[]{:S(2)}) %collective-permute-start.4) | collective-permute-done | bytes 131104 | tf_op jit(solution)/shard_map/ppermute | solution.py:200
  20.8 0.0 collective-permute-start.7
  20.8 0.0 collective-permute-done.3.refs_3_
  20.8 1.7 %collective-permute-start.9 = (bf16[256,256]{1,0:T(8,128)(2,1)S(1)}, bf16[256,256]{1,0:T(8,128)(2,1)S(1)}, u32[]{:S(2)}, u32[]{:S(2)}) collective-permute-start(bf16[256,256]{1,0:T(8,128)(2,1)S(1)} %collective-permute-done.4.refs_4_), channel_id=1, source_target_pairs={{0,2},{1,3},{2,0},{3,1},{4,6},{5,7},{6,4},{7,5},{8,10},{9,11},{10,... | collective-permute-start | bytes 393224 | tf_op jit(solution)/shard_map/ppermute | solution.py:200
  22.5 0.5 %collective-permute-done.13.refs_4_.refs_12_ = bf16[256,256]{1,0:T(8,128)(2,1)S(1)} collective-permute-done((bf16[256,256]{1,0:T(8,128)(2,1)S(1)}, bf16[256,256]{1,0:T(8,128)(2,1)S(1)}, u32[]{:S(2)}, u32[]{:S(2)}) %collective-permute-start.13) | collective-permute-done | bytes 131104 | tf_op jit(solution)/shard_map/ppermute | solution.py:200
  23.1 0.0 collective-permute-start.5
  23.1 0.0 collective-permute-done.11.refs_2_.refs_10_
  23.1 1.7 %collective-permute-start.15 = (bf16[256,256]{1,0:T(8,128)(2,1)S(1)}, bf16[256,256]{1,0:T(8,128)(2,1)S(1)}, u32[]{:S(2)}, u32[]{:S(2)}) collective-permute-start(bf16[256,256]{1,0:T(8,128)(2,1)S(1)} %collective-permute-done.13.refs_4_.refs_12_), channel_id=1, source_target_pairs={{0,2},{1,3},{2,0},{3,1},{4,6},{5,7},{6,4},{7,5},{8,10},{9,11},{10,... | collective-permute-start | bytes 393224 | tf_op jit(solution)/shard_map/ppermute | solution.py:200
  24.8 0.3 scales.1.scale_ref
  25.2 0.0 collective-permute-done.7.refs_7_.refs_9_
  25.2 0.3 collective-permute-start.14
  25.5 1.7 %collective-permute-done.9.refs_0_.refs_6_ = bf16[256,256]{1,0:T(8,128)(2,1)S(1)} collective-permute-done((bf16[256,256]{1,0:T(8,128)(2,1)S(1)}, bf16[256,256]{1,0:T(8,128)(2,1)S(1)}, u32[]{:S(2)}, u32[]{:S(2)}) %collective-permute-start.9) | collective-permute-done | bytes 131104 | tf_op jit(solution)/shard_map/ppermute | solution.py:200
  27.2 0.0 collective-permute-start.12
  27.2 0.0 collective-permute-done.5.refs_5_
  27.2 0.5 collective-permute-start.10
  27.7 1.8 %collective-permute-done.15.refs_0_.refs_14_ = bf16[256,256]{1,0:T(8,128)(2,1)S(1)} collective-permute-done((bf16[256,256]{1,0:T(8,128)(2,1)S(1)}, bf16[256,256]{1,0:T(8,128)(2,1)S(1)}, u32[]{:S(2)}, u32[]{:S(2)}) %collective-permute-start.15) | collective-permute-done | bytes 131104 | tf_op jit(solution)/shard_map/ppermute | solution.py:200
  29.6 0.0 collective-permute-start.16
  29.6 0.0 collective-permute-done.other_ref
  29.6 3.2 %early.1 = (bf16[2048,256]{1,0:T(8,128)(2,1)S(1)}, f32[1152,256]{1,0:T(8,128)S(1)}) custom-call(s32[5]{0:T(128)S(1)} %get-tuple-element.17.count_ref, s32[576]{0:T(1024)S(1)} %get-tuple-element.18.list_ref, bf16[2048,128]{1,0:T(8,128)(2,1)S(1)} %get-tuple-element.19.mine_ref, bf16[2048,128]{1,0:T(8,128)(2,1)S(1)} %collective-permute-done.other_ref, ...), custom_call_target="tpu_custom_call" | custom-call | flops 2147483648 | tf_op jit(solution)/shard_map/early/pallas_call | solution.py:268
  32.8 0.0 collective-permute-done.14.refs_5_.refs_13_
  32.8 0.0 collective-permute-done.12.refs_3_.refs_11_
  32.8 0.0 collective-permute-done.10.refs_1_.refs_7_
  32.8 2.2 %middle.1._ = f32[1152,256]{1,0:T(8,128)S(1)} custom-call(s32[5]{0:T(128)S(1)} %get-tuple-element.17.count_ref, s32[576]{0:T(1024)S(1)} %get-tuple-element.18.list_ref, bf16[2048,256]{1,0:T(8,128)(2,1)S(1)} %get-tuple-element.22.full_ref, bf16[128,128,128]{2,1,0:T(8,128)(2,1)S(1)} %get-tuple-element.20.conf_ref, ...), custom_call_target="tpu_custom_call", output_to_operand_aliasing={{}: (4, {})} | custom-call | flops 1073741824 | tf_op jit(solution)/shard_map/middle/pallas_call | solution.py:278
  35.0 0.0 collective-permute-done.16.refs_1_.refs_15_
  35.0 1.5 %late.1 = (f32[1024,128]{1,0:T(8,128)S(1)}, bf16[1024,128]{1,0:T(8,128)(2,1)S(1)}, f32[1152,256]{1,0:T(8,128)S(1)}) custom-call(s32[5]{0:T(128)S(1)} %get-tuple-element.17.count_ref, s32[576]{0:T(1024)S(1)} %get-tuple-element.18.list_ref, bf16[2048,256]{1,0:T(8,128)(2,1)S(1)} %get-tuple-element.22.full_ref, ...), custom_call_target="tpu_custom_call", output_to_operand_aliasing={{2}: (5, {})} | custom-call | flops 2147483648 | tf_op jit(solution)/shard_map/late/pallas_call | solution.py:289
  36.5 1.7 %collective-permute-start.18 = (bf16[1024,128]{1,0:T(8,128)(2,1)S(1)}, bf16[1024,128]{1,0:T(8,128)(2,1)S(1)}, u32[]{:S(2)}, u32[]{:S(2)}) collective-permute-start(bf16[1024,128]{1,0:T(8,128)(2,1)S(1)} %get-tuple-element.28), channel_id=1, source_target_pairs={{0,16},{16,0},{1,17},{17,1},{2,18},{18,2},{3,19},{19,3},{4,20},{20... | collective-permute-start | bytes 786440 | tf_op jit(solution)/shard_map/ppermute | solution.py:300
  38.2 3.9 %second.1 = (f32[1024,128]{1,0:T(8,128)S(1)}, bf16[1024,128]{1,0:T(8,128)(2,1)S(1)}) custom-call(s32[5]{0:T(128)S(1)} %get-tuple-element.17.count_ref, s32[576]{0:T(1024)S(1)} %get-tuple-element.18.list_ref, bf16[2048,256]{1,0:T(8,128)(2,1)S(1)} %get-tuple-element.22.full_ref, f32[2048,128]{1,0:T(8,128)S(1)} %scales.1.scale_ref, ...), custom_call_target="tpu_custom_call" | custom-call | flops 2147483648 | tf_op jit(solution)/shard_map/second/pallas_call | solution.py:301
  42.2 1.2 %collective-permute-start.17 = (bf16[1024,128]{1,0:T(8,128)(2,1)S(1)}, bf16[1024,128]{1,0:T(8,128)(2,1)S(1)}, u32[]{:S(2)}, u32[]{:S(2)}) collective-permute-start(bf16[1024,128]{1,0:T(8,128)(2,1)S(1)} %get-tuple-element.27), channel_id=1, source_target_pairs={{0,16},{16,0},{1,17},{17,1},{2,18},{18,2},{3,19},{19,3},{4,20},{20... | collective-permute-start | bytes 786440 | tf_op jit(solution)/shard_map/ppermute | solution.py:311
  43.3 1.3 %collective-permute-done.18.came_ref = bf16[1024,128]{1,0:T(8,128)(2,1)S(1)} collective-permute-done((bf16[1024,128]{1,0:T(8,128)(2,1)S(1)}, bf16[1024,128]{1,0:T(8,128)(2,1)S(1)}, u32[]{:S(2)}, u32[]{:S(2)}) %collective-permute-start.18) | collective-permute-done | bytes 262176 | tf_op jit(solution)/shard_map/ppermute | solution.py:300
  44.6 0.7 %shard_map.55.refs_0_ = bf16[2048,128]{1,0:T(8,128)(2,1)} custom-call(f32[1024,128]{1,0:T(8,128)S(1)} %get-tuple-element.25._.keep_ref, bf16[1024,128]{1,0:T(8,128)(2,1)S(1)} %collective-permute-done.18.came_ref), custom_call_target="tpu_custom_call" | custom-call | tf_op jit(solution)/shard_map/pallas_call | solution.py:314
  45.3 5.3 %collective-permute-done.17.came_ref = bf16[1024,128]{1,0:T(8,128)(2,1)S(1)} collective-permute-done((bf16[1024,128]{1,0:T(8,128)(2,1)S(1)}, bf16[1024,128]{1,0:T(8,128)(2,1)S(1)}, u32[]{:S(2)}, u32[]{:S(2)}) %collective-permute-start.17) | collective-permute-done | bytes 262176 | tf_op jit(solution)/shard_map/ppermute | solution.py:311
  50.6 0.8 %shard_map.56 = bf16[2048,128]{1,0:T(8,128)(2,1)} custom-call(f32[1024,128]{1,0:T(8,128)S(1)} %get-tuple-element.26.keep_ref, bf16[1024,128]{1,0:T(8,128)(2,1)S(1)} %collective-permute-done.17.came_ref, bf16[2048,128]{1,0:T(8,128)(2,1)} %shard_map.55.refs_0_), custom_call_target="tpu_custom_call", output_to_operand_aliasing={{}: (2, {})} | custom-call | tf_op jit(solution)/shard_map/pallas_call | solution.py:314
Async XLA Ops:
  0.0 29.6 %collective-permute-start = (bf16[2048,128]{1,0:T(8,128)(2,1)}, bf16[2048,128]{1,0:T(8,128)(2,1)S(1)}, u32[]{:S(2)}, u32[]{:S(2)}) collective-permute-start(bf16[2048,128]{1,0:T(8,128)(2,1)} %mine_hbm.1), channel_id=1, source_target_pairs={{0,16},{16,0},{1,17},{17,1},{2,18},{18,2},{3,19},{19,3},{4,20},{20... | collective-permute-start | bytes 1572872 | tf_op jit(solution)/shard_map/ppermute | solution.py:224
  3.0 14.1 %collective-permute-start.2 = (bf16[256,256]{1,0:T(8,128)(2,1)}, bf16[256,256]{1,0:T(8,128)(2,1)S(1)}, u32[]{:S(2)}, u32[]{:S(2)}) collective-permute-start(bf16[256,256]{1,0:T(8,128)(2,1)} %own_hbm.1), channel_id=1, source_target_pairs={{0,2},{1,3},{2,0},{3,1},{4,6},{5,7},{6,4},{7,5},{8,10},{9,11},{10,... | collective-permute-start | bytes 393224 | tf_op jit(solution)/shard_map/ppermute | solution.py:200
  4.5 12.6 %collective-permute-start.6 = (bf16[256,256]{1,0:T(8,128)(2,1)}, bf16[256,256]{1,0:T(8,128)(2,1)S(1)}, u32[]{:S(2)}, u32[]{:S(2)}) collective-permute-start(bf16[256,256]{1,0:T(8,128)(2,1)} %own_hbm.1), channel_id=1, source_target_pairs={{0,8},{1,9},{2,10},{3,11},{4,12},{5,13},{6,14},{7,15},{8,0},{9,1},... | collective-permute-start | bytes 393224 | tf_op jit(solution)/shard_map/ppermute | solution.py:200
  7.1 10.3 %collective-permute-start.1 = (bf16[256,256]{1,0:T(8,128)(2,1)}, bf16[256,256]{1,0:T(8,128)(2,1)S(1)}, u32[]{:S(2)}, u32[]{:S(2)}) collective-permute-start(bf16[256,256]{1,0:T(8,128)(2,1)} %own_hbm.1), channel_id=1, source_target_pairs={{0,1},{1,0},{2,3},{3,2},{4,5},{5,4},{6,7},{7,6},{8,9},{9,8},{10,11... | collective-permute-start | bytes 393224 | tf_op jit(solution)/shard_map/ppermute | solution.py:200
  7.1 8.2 %copy-start = (bf16[256,256]{1,0:T(8,128)(2,1)S(1)}, bf16[256,256]{1,0:T(8,128)(2,1)}, u32[]{:S(2)}) copy-start(bf16[256,256]{1,0:T(8,128)(2,1)} %own_hbm.1) | copy-start | bytes 393220
  10.5 4.8 %collective-permute-start.8 = (f32[16,128]{1,0:T(8,128)S(1)}, f32[16,128]{1,0:T(8,128)S(1)}, u32[]{:S(2)}, u32[]{:S(2)}) collective-permute-start(f32[16,128]{1,0:T(8,128)S(1)} %get-tuple-element.23.mine_ref), channel_id=1, source_target_pairs={{0,16},{16,0},{1,17},{17,1},{2,18},{18,2},{3,19},{19,3},{4,20},{20... | collective-permute-start | bytes 24584 | tf_op jit(solution)/shard_map/ppermute | solution.py:255
  15.3 5.6 %collective-permute-start.4 = (bf16[256,256]{1,0:T(8,128)(2,1)S(1)}, bf16[256,256]{1,0:T(8,128)(2,1)S(1)}, u32[]{:S(2)}, u32[]{:S(2)}) collective-permute-start(bf16[256,256]{1,0:T(8,128)(2,1)S(1)} %copy-done), channel_id=1, source_target_pairs={{0,4},{1,5},{2,6},{3,7},{4,0},{5,1},{6,2},{7,3},{8,12},{9,13},{10,... | collective-permute-start | bytes 393224 | tf_op jit(solution)/shard_map/ppermute | solution.py:200
  17.1 3.7 %collective-permute-start.3 = (bf16[256,256]{1,0:T(8,128)(2,1)S(1)}, bf16[256,256]{1,0:T(8,128)(2,1)S(1)}, u32[]{:S(2)}, u32[]{:S(2)}) collective-permute-start(bf16[256,256]{1,0:T(8,128)(2,1)S(1)} %collective-permute-done.2.refs_2_), channel_id=1, source_target_pairs={{0,1},{1,0},{2,3},{3,2},{4,5},{5,4},{6,7},{7,6},{8,9},{9,8},{10,11... | collective-permute-start | bytes 393224 | tf_op jit(solution)/shard_map/ppermute | solution.py:200
  17.1 5.9 %collective-permute-start.13 = (bf16[256,256]{1,0:T(8,128)(2,1)S(1)}, bf16[256,256]{1,0:T(8,128)(2,1)S(1)}, u32[]{:S(2)}, u32[]{:S(2)}) collective-permute-start(bf16[256,256]{1,0:T(8,128)(2,1)S(1)} %collective-permute-done.6.refs_6_.refs_8_), channel_id=1, source_target_pairs={{0,4},{1,5},{2,6},{3,7},{4,0},{5,1},{6,2},{7,3},{8,12},{9,13},{10,... | collective-permute-start | bytes 393224 | tf_op jit(solution)/shard_map/ppermute | solution.py:200
  17.4 5.7 %collective-permute-start.11 = (bf16[256,256]{1,0:T(8,128)(2,1)S(1)}, bf16[256,256]{1,0:T(8,128)(2,1)S(1)}, u32[]{:S(2)}, u32[]{:S(2)}) collective-permute-start(bf16[256,256]{1,0:T(8,128)(2,1)S(1)} %collective-permute-done.6.refs_6_.refs_8_), channel_id=1, source_target_pairs={{0,2},{1,3},{2,0},{3,1},{4,6},{5,7},{6,4},{7,5},{8,10},{9,11},{10,... | collective-permute-start | bytes 393224 | tf_op jit(solution)/shard_map/ppermute | solution.py:200
  20.8 4.4 %collective-permute-start.7 = (bf16[256,256]{1,0:T(8,128)(2,1)S(1)}, bf16[256,256]{1,0:T(8,128)(2,1)S(1)}, u32[]{:S(2)}, u32[]{:S(2)}) collective-permute-start(bf16[256,256]{1,0:T(8,128)(2,1)S(1)} %collective-permute-done.6.refs_6_.refs_8_), channel_id=1, source_target_pairs={{0,1},{1,0},{2,3},{3,2},{4,5},{5,4},{6,7},{7,6},{8,9},{9,8},{10,11... | collective-permute-start | bytes 393224 | tf_op jit(solution)/shard_map/ppermute | solution.py:200
  20.8 6.4 %collective-permute-start.9 = (bf16[256,256]{1,0:T(8,128)(2,1)S(1)}, bf16[256,256]{1,0:T(8,128)(2,1)S(1)}, u32[]{:S(2)}, u32[]{:S(2)}) collective-permute-start(bf16[256,256]{1,0:T(8,128)(2,1)S(1)} %collective-permute-done.4.refs_4_), channel_id=1, source_target_pairs={{0,2},{1,3},{2,0},{3,1},{4,6},{5,7},{6,4},{7,5},{8,10},{9,11},{10,... | collective-permute-start | bytes 393224 | tf_op jit(solution)/shard_map/ppermute | solution.py:200
  23.1 4.2 %collective-permute-start.5 = (bf16[256,256]{1,0:T(8,128)(2,1)S(1)}, bf16[256,256]{1,0:T(8,128)(2,1)S(1)}, u32[]{:S(2)}, u32[]{:S(2)}) collective-permute-start(bf16[256,256]{1,0:T(8,128)(2,1)S(1)} %collective-permute-done.4.refs_4_), channel_id=1, source_target_pairs={{0,1},{1,0},{2,3},{3,2},{4,5},{5,4},{6,7},{7,6},{8,9},{9,8},{10,11... | collective-permute-start | bytes 393224 | tf_op jit(solution)/shard_map/ppermute | solution.py:200
  23.1 6.5 %collective-permute-start.15 = (bf16[256,256]{1,0:T(8,128)(2,1)S(1)}, bf16[256,256]{1,0:T(8,128)(2,1)S(1)}, u32[]{:S(2)}, u32[]{:S(2)}) collective-permute-start(bf16[256,256]{1,0:T(8,128)(2,1)S(1)} %collective-permute-done.13.refs_4_.refs_12_), channel_id=1, source_target_pairs={{0,2},{1,3},{2,0},{3,1},{4,6},{5,7},{6,4},{7,5},{8,10},{9,11},{10,... | collective-permute-start | bytes 393224 | tf_op jit(solution)/shard_map/ppermute | solution.py:200
  25.2 7.6 %collective-permute-start.14 = (bf16[256,256]{1,0:T(8,128)(2,1)S(1)}, bf16[256,256]{1,0:T(8,128)(2,1)S(1)}, u32[]{:S(2)}, u32[]{:S(2)}) collective-permute-start(bf16[256,256]{1,0:T(8,128)(2,1)S(1)} %collective-permute-done.13.refs_4_.refs_12_), channel_id=1, source_target_pairs={{0,1},{1,0},{2,3},{3,2},{4,5},{5,4},{6,7},{7,6},{8,9},{9,8},{10,11... | collective-permute-start | bytes 393224 | tf_op jit(solution)/shard_map/ppermute | solution.py:200
  27.2 5.6 %collective-permute-start.12 = (bf16[256,256]{1,0:T(8,128)(2,1)S(1)}, bf16[256,256]{1,0:T(8,128)(2,1)S(1)}, u32[]{:S(2)}, u32[]{:S(2)}) collective-permute-start(bf16[256,256]{1,0:T(8,128)(2,1)S(1)} %collective-permute-done.11.refs_2_.refs_10_), channel_id=1, source_target_pairs={{0,1},{1,0},{2,3},{3,2},{4,5},{5,4},{6,7},{7,6},{8,9},{9,8},{10,11... | collective-permute-start | bytes 393224 | tf_op jit(solution)/shard_map/ppermute | solution.py:200
  27.2 5.6 %collective-permute-start.10 = (bf16[256,256]{1,0:T(8,128)(2,1)S(1)}, bf16[256,256]{1,0:T(8,128)(2,1)S(1)}, u32[]{:S(2)}, u32[]{:S(2)}) collective-permute-start(bf16[256,256]{1,0:T(8,128)(2,1)S(1)} %collective-permute-done.9.refs_0_.refs_6_), channel_id=1, source_target_pairs={{0,1},{1,0},{2,3},{3,2},{4,5},{5,4},{6,7},{7,6},{8,9},{9,8},{10,11... | collective-permute-start | bytes 393224 | tf_op jit(solution)/shard_map/ppermute | solution.py:200
  29.6 5.4 %collective-permute-start.16 = (bf16[256,256]{1,0:T(8,128)(2,1)S(1)}, bf16[256,256]{1,0:T(8,128)(2,1)S(1)}, u32[]{:S(2)}, u32[]{:S(2)}) collective-permute-start(bf16[256,256]{1,0:T(8,128)(2,1)S(1)} %collective-permute-done.15.refs_0_.refs_14_), channel_id=1, source_target_pairs={{0,1},{1,0},{2,3},{3,2},{4,5},{5,4},{6,7},{7,6},{8,9},{9,8},{10,11... | collective-permute-start | bytes 393224 | tf_op jit(solution)/shard_map/ppermute | solution.py:200
  36.5 8.1 %collective-permute-start.18 = (bf16[1024,128]{1,0:T(8,128)(2,1)S(1)}, bf16[1024,128]{1,0:T(8,128)(2,1)S(1)}, u32[]{:S(2)}, u32[]{:S(2)}) collective-permute-start(bf16[1024,128]{1,0:T(8,128)(2,1)S(1)} %get-tuple-element.28), channel_id=1, source_target_pairs={{0,16},{16,0},{1,17},{17,1},{2,18},{18,2},{3,19},{19,3},{4,20},{20... | collective-permute-start | bytes 786440 | tf_op jit(solution)/shard_map/ppermute | solution.py:300
  42.2 8.5 %collective-permute-start.17 = (bf16[1024,128]{1,0:T(8,128)(2,1)S(1)}, bf16[1024,128]{1,0:T(8,128)(2,1)S(1)}, u32[]{:S(2)}, u32[]{:S(2)}) collective-permute-start(bf16[1024,128]{1,0:T(8,128)(2,1)S(1)} %get-tuple-element.27), channel_id=1, source_target_pairs={{0,16},{16,0},{1,17},{17,1},{2,18},{18,2},{3,19},{19,3},{4,20},{20... | collective-permute-start | bytes 786440 | tf_op jit(solution)/shard_map/ppermute | solution.py:311

commit v4 on v3

--- a/solution.py
+++ b/solution.py
@@ -28,7 +28,7 @@
     return jnp.where(one, 0, jnp.where(chip == n_blk // 2 - 1, 2, 1))
 
 
-def prepare(n_blk, per, spare, users_hbm, items_hbm, conf_hbm, mine_hbm, own_hbm, sums_ref, conf_ref, mine_ref, own_ref, list_ref, count_ref, users_ref, items_ref, table_ref, ends_ref, acc_ref, sems):
+def prepare(n_blk, per, spare, users_hbm, items_hbm, conf_hbm, mine_hbm, own_hbm, sums_ref, conf_ref, mine_ref, own_ref, list_ref, count_ref, zero1_ref, zero2_ref, users_ref, items_ref, table_ref, ends_ref, acc_ref, sems):
     tiles, _, _ = conf_ref.shape
     blocks = sums_ref.shape[0]
     parts = sems.shape[0] - 4
@@ -51,7 +51,8 @@
         conf_copy(i).start()
     for c in later:
         c.start()
-    acc_ref[...] = jnp.zeros_like(acc_ref)
+    for ref in (acc_ref, zero1_ref, zero2_ref):
+        ref[...] = jnp.zeros_like(ref)
     for item in range(table_ref.shape[0]):
         slot = item // per ^ me
         table_ref[item] = (stage_of(slot, n_blk) << SLOT_BITS) + slot * per + item % per
@@ -130,7 +131,7 @@
             item_ref[s * per + j] = ref[j * tb : (j + 1) * tb, :]
 
 
-def early(places, count_ref, list_ref, mine_ref, other_ref, conf_ref, *refs):
+def early(places, count_ref, list_ref, mine_ref, other_ref, conf_ref, _, *refs):
     slot_refs = refs[: len(places)]
     full_ref, acc_ref, item_ref, w_ref = refs[len(places) :]
     half = mine_ref.shape[1]
@@ -139,7 +140,6 @@
     full_ref[:, pl.ds(here, half)] = mine_ref[...]
     full_ref[:, pl.ds(there, half)] = other_ref[...]
     fill(item_ref, slot_refs, places)
-    acc_ref[...] = jnp.zeros_like(acc_ref)
     run_tiles(0, count_ref[0], 0, list_ref, full_ref, item_ref, conf_ref, w_ref, acc_ref)
 
 
@@ -152,7 +152,7 @@
     keep_ref[...] = acc_ref[:rows, pl.ds(here, half)] * scale
 
 
-def middle(places, count_ref, list_ref, full_ref, conf_ref, _, *refs):
+def middle(places, count_ref, list_ref, full_ref, conf_ref, _, __, *refs):
     slot_refs = refs[: len(places)]
     acc_ref, item_ref, w_ref = refs[len(places) :]
     base = list_ref.shape[0] // 4
@@ -160,7 +160,7 @@
     run_tiles(base, count_ref[1], 0, list_ref, full_ref, item_ref, conf_ref, w_ref, acc_ref)
 
 
-def late(places, count_ref, list_ref, full_ref, scale_ref, conf_ref, _, *refs):
+def late(places, count_ref, list_ref, full_ref, scale_ref, conf_ref, _, __, *refs):
     slot_refs = refs[: len(places)]
     keep_ref, send_ref, acc_ref, item_ref, w_ref = refs[len(places) :]
     base = list_ref.shape[0] // 4
@@ -169,13 +169,9 @@
     finish(keep_ref, send_ref, acc_ref, scale_ref, count_ref[4], 0)
 
 
-def second(places, count_ref, list_ref, full_ref, scale_ref, conf_ref, _, *refs):
-    slot_refs = refs[: len(places)]
-    keep_ref, send_ref, acc_ref, item_ref, w_ref = refs[len(places) :]
+def second(count_ref, list_ref, full_ref, scale_ref, conf_ref, item_ref, _, __, keep_ref, send_ref, acc_ref, w_ref):
     rows = keep_ref.shape[0]
     base = list_ref.shape[0] // 4
-    fill(item_ref, slot_refs, places)
-    acc_ref[...] = jnp.zeros_like(acc_ref)
     block = rows // conf_ref.shape[1]
     run_tiles(3 * base, count_ref[3], block, list_ref, full_ref, item_ref, conf_ref, w_ref, acc_ref)
     finish(keep_ref, send_ref, acc_ref, scale_ref, count_ref[4], rows)
@@ -227,8 +223,9 @@
     for d in range(n_blk):
         chip = d >> 1
         places[0 if chip & (chip - 1) == 0 else 2 if chip == n_blk // 2 - 1 else 1].append(d)
+    acc_shape = jax.ShapeDtypeStruct((rows // 2 + tb, 2 * half), F32)
     hbm = [pltpu.with_memory_space_constraint(x, pltpu.HBM) for x in (user_list, item_list, conf, users, items)]
-    sums, conf_v, mine, slots[0], order, count = pl.pallas_call(
+    sums, conf_v, mine, slots[0], order, count, acc, acc2 = pl.pallas_call(
         functools.partial(prepare, n_blk, per, places[1][0]),
         out_shape=(
             jax.ShapeDtypeStruct((blocks, tb), F32),
@@ -237,9 +234,11 @@
             jax.ShapeDtypeStruct(items.shape, BF16),
             jax.ShapeDtypeStruct((4 * (tiles + STEP),), I32),
             jax.ShapeDtypeStruct((5,), I32),
+            acc_shape,
+            acc_shape,
         ),
         in_specs=[HBM] * 5,
-        out_specs=(VM, VM, VM, VM, SM, SM),
+        out_specs=(VM, VM, VM, VM, SM, SM, VM, VM),
         scratch_shapes=[
             pltpu.SMEM((tiles,), I32),
             pltpu.SMEM((tiles,), I32),
@@ -261,53 +260,55 @@
         compiler_params=params(2),
         name="scales",
     )(sums, sums_other)
-    scratch = [pltpu.VMEM((n_blk * per, tb, 2 * half), BF16), pltpu.VMEM((STEP, tb, tb), BF16)]
-    acc_shape = jax.ShapeDtypeStruct((rows // 2 + tb, 2 * half), F32)
+    scratch = [pltpu.VMEM((STEP, tb, tb), BF16)]
+    gathered = jax.ShapeDtypeStruct((n_blk * per, tb, 2 * half), BF16)
     half_shapes = (jax.ShapeDtypeStruct((rows // 2, half), F32), jax.ShapeDtypeStruct((rows // 2, half), BF16))
     scalars = (count, order)
-    full, acc = pl.pallas_call(
+    full, acc, all_items = pl.pallas_call(
         functools.partial(early, places[0]),
-        out_shape=(jax.ShapeDtypeStruct((rows, 2 * half), BF16), acc_shape),
-        in_specs=[SM] * 2 + [VM] * (3 + len(places[0])),
-        out_specs=(VM, VM),
+        out_shape=(jax.ShapeDtypeStruct((rows, 2 * half), BF16), acc_shape, gathered),
+        in_specs=[SM] * 2 + [VM] * (4 + len(places[0])),
+        out_specs=(VM, VM, VM),
         scratch_shapes=scratch,
+        input_output_aliases={5: 1},
         compiler_params=params(TILE_MIB),
         cost_estimate=pl.CostEstimate(flops=tiles * tb * tb * half * 8, bytes_accessed=0, transcendentals=0),
         name="early",
-    )(*scalars, mine, other, conf_v, *[slots[d] for d in places[0]])
-    acc = pl.pallas_call(
+    )(*scalars, mine, other, conf_v, acc, *[slots[d] for d in places[0]])
+    acc, all_items = pl.pallas_call(
         functools.partial(middle, places[1]),
-        out_shape=acc_shape,
-        in_specs=[SM] * 2 + [VM] * (3 + len(places[1])),
-        out_specs=VM,
+        out_shape=(acc_shape, gathered),
+        in_specs=[SM] * 2 + [VM] * (4 + len(places[1])),
+        out_specs=(VM, VM),
         scratch_shapes=scratch,
-        input_output_aliases={4: 0},
+        input_output_aliases={4: 0, 5: 1},
         compiler_params=params(TILE_MIB),
         cost_estimate=pl.CostEstimate(flops=tiles * tb * tb * half * 4, bytes_accessed=0, transcendentals=0),
         name="middle",
-    )(*scalars, full, conf_v, acc, *[slots[d] for d in places[1]])
-    keep, send, _ = pl.pallas_call(
+    )(*scalars, full, conf_v, acc, all_items, *[slots[d] for d in places[1]])
+    keep, send, _, all_items = pl.pallas_call(
         functools.partial(late, places[2]),
-        out_shape=(*half_shapes, acc_shape),
-        in_specs=[SM] * 2 + [VM] * (4 + len(places[2])),
-        out_specs=(VM, VM, VM),
+        out_shape=(*half_shapes, acc_shape, gathered),
+        in_specs=[SM] * 2 + [VM] * (5 + len(places[2])),
+        out_specs=(VM, VM, VM, VM),
         scratch_shapes=scratch,
-        input_output_aliases={5: 2},
+        input_output_aliases={5: 2, 6: 3},
         compiler_params=params(TILE_MIB),
         cost_estimate=pl.CostEstimate(flops=tiles * tb * tb * half * 8, bytes_accessed=0, transcendentals=0),
         name="late",
-    )(*scalars, full, scale, conf_v, acc, *[slots[d] for d in places[2]])
+    )(*scalars, full, scale, conf_v, acc, all_items, *[slots[d] for d in places[2]])
     arrived = lax.ppermute(send, "fiber", swap_fiber)
-    keep2, send2 = pl.pallas_call(
-        functools.partial(second, range(n_blk)),
-        out_shape=half_shapes,
-        in_specs=[SM] * 2 + [VM] * (4 + n_blk),
-        out_specs=(VM, VM),
-        scratch_shapes=[pltpu.VMEM(acc_shape.shape, F32)] + scratch,
+    keep2, send2, _ = pl.pallas_call(
+        second,
+        out_shape=(*half_shapes, acc_shape),
+        in_specs=[SM] * 2 + [VM] * 6,
+        out_specs=(VM, VM, VM),
+        scratch_shapes=scratch,
+        input_output_aliases={6: 2},
         compiler_params=params(TILE_MIB),
         cost_estimate=pl.CostEstimate(flops=tiles * tb * tb * half * 8, bytes_accessed=0, transcendentals=0),
         name="second",
-    )(*scalars, full, scale, conf_v, keep, *slots)
+    )(*scalars, full, scale, conf_v, all_items, acc2, keep)
     arrived2 = lax.ppermute(send2, "fiber", swap_fiber)
     out = None
     for i, (kept, came) in enumerate(((keep, arrived), (keep2, arrived2))):

time: 51.5 us -> 51.3 us (level)
  no operation moved by 1% of the time
where the time goes in v4:
time: 51.3 us; the launch traced here: 51.1 us
  starting transfers between devices  18.7 us (36%)
  waiting for transfers between devices  16.5 us (32%)
  Pallas kernels  15.9 us (31%)
    ppermute x15, starting transfers between devices, swap(): return lax.ppermute(x, 'blk', [(i, i ^ bits) for i in range(n_blk)])  12.2 us
    ppermute x15, waiting for transfers between devices, swap(): return lax.ppermute(x, 'blk', [(i, i ^ bits) for i in range(n_blk)])  5.83 us
    ppermute x1, waiting for transfers between devices, shards(): arrived2 = lax.ppermute(send2, 'fiber', swap_fiber)  5.04 us
    ppermute x1, waiting for transfers between devices, shards(): sums_other = lax.ppermute(sums, 'fiber', swap_fiber)  4.11 us
    pallas_call x1, Pallas kernels, shards(): pl.pallas_call(second, out_shape=(*half_shapes, acc_shape), in_specs=[SM]...  3.78 us
    pallas_call x1, Pallas kernels, shards(): pl.pallas_call(functools.partial(prepare, n_blk, per, places[1][0]), out_...  3.47 us
    pallas_call x1, Pallas kernels, shards(): pl.pallas_call(functools.partial(early, places[0]), out_shape=(jax.ShapeD...  3.11 us
    ppermute x1, starting transfers between devices, shards(): other = lax.ppermute(users, 'fiber', swap_fiber)  2.97 us
  transfers between devices with their start and end apart: 19, of which 7 were waited for; matrix products, arithmetic and copies ran while one was open for 0% of the time, Pallas kernels for 27%

profile of v4, /device:TPU:0, one launch (start us, length us, event | category | flops | bytes accessed | tf_op | source)
XLA Modules:
  0.0 51.1 jit_solution(5942291447222125853)
XLA Ops:
  0.0 3.0 %collective-permute-start = (bf16[2048,128]{1,0:T(8,128)(2,1)}, bf16[2048,128]{1,0:T(8,128)(2,1)S(1)}, u32[]{:S(2)}, u32[]{:S(2)}) collective-permute-start(bf16[2048,128]{1,0:T(8,128)(2,1)} %mine_hbm.1), channel_id=1, source_target_pairs={{0,16},{16,0},{1,17},{17,1},{2,18},{18,2},{3,19},{19,3},{4,20},{20... | collective-permute-start | bytes 1572872 | tf_op jit(solution)/shard_map/ppermute | solution.py:220
  3.0 1.5 %collective-permute-start.2 = (bf16[256,256]{1,0:T(8,128)(2,1)}, bf16[256,256]{1,0:T(8,128)(2,1)S(1)}, u32[]{:S(2)}, u32[]{:S(2)}) collective-permute-start(bf16[256,256]{1,0:T(8,128)(2,1)} %own_hbm.1), channel_id=1, source_target_pairs={{0,2},{1,3},{2,0},{3,1},{4,6},{5,7},{6,4},{7,5},{8,10},{9,11},{10,... | collective-permute-start | bytes 393224 | tf_op jit(solution)/shard_map/ppermute | solution.py:196
  4.5 2.6 %collective-permute-start.6 = (bf16[256,256]{1,0:T(8,128)(2,1)}, bf16[256,256]{1,0:T(8,128)(2,1)S(1)}, u32[]{:S(2)}, u32[]{:S(2)}) collective-permute-start(bf16[256,256]{1,0:T(8,128)(2,1)} %own_hbm.1), channel_id=1, source_target_pairs={{0,8},{1,9},{2,10},{3,11},{4,12},{5,13},{6,14},{7,15},{8,0},{9,1},... | collective-permute-start | bytes 393224 | tf_op jit(solution)/shard_map/ppermute | solution.py:196
  7.1 0.0 collective-permute-start.1
  7.1 0.0 copy-start
  7.1 3.5 %prepare.1 = (f32[16,128]{1,0:T(8,128)S(1)}, bf16[128,128,128]{2,1,0:T(8,128)(2,1)S(1)}, bf16[2048,128]{1,0:T(8,128)(2,1)S(1)}, bf16[256,256]{1,0:T(8,128)(2,1)S...) custom-call(s32[128]{0:T(128)} %bitcast.4, s32[128]{0:T(128)} %bitcast.5, ...), custom_call_target="tpu_custom_call" | custom-call | bytes 8388608 | tf_op jit(solution)/shard_map/prepare/pallas_call | solution.py:228
  10.6 0.6 %collective-permute-start.8 = (f32[16,128]{1,0:T(8,128)S(1)}, f32[16,128]{1,0:T(8,128)S(1)}, u32[]{:S(2)}, u32[]{:S(2)}) collective-permute-start(f32[16,128]{1,0:T(8,128)S(1)} %get-tuple-element.30.mine_ref), channel_id=1, source_target_pairs={{0,16},{16,0},{1,17},{17,1},{2,18},{18,2},{3,19},{19,3},{4,20},{20... | collective-permute-start | bytes 24584 | tf_op jit(solution)/shard_map/ppermute | solution.py:254
  11.2 4.1 %collective-permute-done.8.other_ref = f32[16,128]{1,0:T(8,128)S(1)} collective-permute-done((f32[16,128]{1,0:T(8,128)S(1)}, f32[16,128]{1,0:T(8,128)S(1)}, u32[]{:S(2)}, u32[]{:S(2)}) %collective-permute-start.8) | collective-permute-done | bytes 8224 | tf_op jit(solution)/shard_map/ppermute | solution.py:254
  15.3 0.0 copy-done
  15.3 1.8 %collective-permute-start.4 = (bf16[256,256]{1,0:T(8,128)(2,1)S(1)}, bf16[256,256]{1,0:T(8,128)(2,1)S(1)}, u32[]{:S(2)}, u32[]{:S(2)}) collective-permute-start(bf16[256,256]{1,0:T(8,128)(2,1)S(1)} %copy-done), channel_id=1, source_target_pairs={{0,4},{1,5},{2,6},{3,7},{4,0},{5,1},{6,2},{7,3},{8,12},{9,13},{10,... | collective-permute-start | bytes 393224 | tf_op jit(solution)/shard_map/ppermute | solution.py:196
  17.1 0.0 collective-permute-done.2.refs_2_
  17.1 0.0 collective-permute-start.3
  17.1 0.0 collective-permute-done.6.refs_6_
  17.1 0.3 collective-permute-start.13
  17.4 0.0 collective-permute-done.1.refs_1_
  17.4 1.8 %collective-permute-start.11 = (bf16[256,256]{1,0:T(8,128)(2,1)S(1)}, bf16[256,256]{1,0:T(8,128)(2,1)S(1)}, u32[]{:S(2)}, u32[]{:S(2)}) collective-permute-start(bf16[256,256]{1,0:T(8,128)(2,1)S(1)} %collective-permute-done.6.refs_6_), channel_id=1, source_target_pairs={{0,2},{1,3},{2,0},{3,1},{4,6},{5,7},{6,4},{7,5},{8,10},{9,11},{10,... | collective-permute-start | bytes 393224 | tf_op jit(solution)/shard_map/ppermute | solution.py:196
  19.2 1.7 %collective-permute-done.4.refs_4_ = bf16[256,256]{1,0:T(8,128)(2,1)S(1)} collective-permute-done((bf16[256,256]{1,0:T(8,128)(2,1)S(1)}, bf16[256,256]{1,0:T(8,128)(2,1)S(1)}, u32[]{:S(2)}, u32[]{:S(2)}) %collective-permute-start.4) | collective-permute-done | bytes 131104 | tf_op jit(solution)/shard_map/ppermute | solution.py:196
  20.8 0.0 collective-permute-start.7
  20.8 0.0 collective-permute-done.3.refs_3_
  20.8 1.7 %collective-permute-start.9 = (bf16[256,256]{1,0:T(8,128)(2,1)S(1)}, bf16[256,256]{1,0:T(8,128)(2,1)S(1)}, u32[]{:S(2)}, u32[]{:S(2)}) collective-permute-start(bf16[256,256]{1,0:T(8,128)(2,1)S(1)} %collective-permute-done.4.refs_4_), channel_id=1, source_target_pairs={{0,2},{1,3},{2,0},{3,1},{4,6},{5,7},{6,4},{7,5},{8,10},{9,11},{10,... | collective-permute-start | bytes 393224 | tf_op jit(solution)/shard_map/ppermute | solution.py:196
  22.5 0.5 %collective-permute-done.13.refs_4_ = bf16[256,256]{1,0:T(8,128)(2,1)S(1)} collective-permute-done((bf16[256,256]{1,0:T(8,128)(2,1)S(1)}, bf16[256,256]{1,0:T(8,128)(2,1)S(1)}, u32[]{:S(2)}, u32[]{:S(2)}) %collective-permute-start.13) | collective-permute-done | bytes 131104 | tf_op jit(solution)/shard_map/ppermute | solution.py:196
  23.1 0.0 collective-permute-start.5
  23.1 0.0 collective-permute-done.11.refs_2_
  23.1 1.7 %collective-permute-start.15 = (bf16[256,256]{1,0:T(8,128)(2,1)S(1)}, bf16[256,256]{1,0:T(8,128)(2,1)S(1)}, u32[]{:S(2)}, u32[]{:S(2)}) collective-permute-start(bf16[256,256]{1,0:T(8,128)(2,1)S(1)} %collective-permute-done.13.refs_4_), channel_id=1, source_target_pairs={{0,2},{1,3},{2,0},{3,1},{4,6},{5,7},{6,4},{7,5},{8,10},{9,11},{10,... | collective-permute-start | bytes 393224 | tf_op jit(solution)/shard_map/ppermute | solution.py:196
  24.8 0.3 scales.1.scale_ref
  25.2 0.0 collective-permute-done.7.refs_7_
  25.2 0.3 collective-permute-start.14
  25.5 1.7 %collective-permute-done.9.refs_0_ = bf16[256,256]{1,0:T(8,128)(2,1)S(1)} collective-permute-done((bf16[256,256]{1,0:T(8,128)(2,1)S(1)}, bf16[256,256]{1,0:T(8,128)(2,1)S(1)}, u32[]{:S(2)}, u32[]{:S(2)}) %collective-permute-start.9) | collective-permute-done | bytes 131104 | tf_op jit(solution)/shard_map/ppermute | solution.py:196
  27.2 0.0 collective-permute-start.12
  27.2 0.0 collective-permute-done.5.refs_5_
  27.2 0.5 collective-permute-start.10
  27.7 1.8 %collective-permute-done.15.refs_0_ = bf16[256,256]{1,0:T(8,128)(2,1)S(1)} collective-permute-done((bf16[256,256]{1,0:T(8,128)(2,1)S(1)}, bf16[256,256]{1,0:T(8,128)(2,1)S(1)}, u32[]{:S(2)}, u32[]{:S(2)}) %collective-permute-start.15) | collective-permute-done | bytes 131104 | tf_op jit(solution)/shard_map/ppermute | solution.py:196
  29.6 0.0 collective-permute-start.16
  29.6 0.0 collective-permute-done.other_ref
  29.6 3.1 %early.1 = (bf16[2048,256]{1,0:T(8,128)(2,1)S(1)}, f32[1152,256]{1,0:T(8,128)S(1)}, bf16[32,128,256]{2,1,0:T(8,128)(2,1)S(1)}) custom-call(s32[5]{0:T(128)S(1)} %get-tuple-element.23.count_ref, s32[576]{0:T(1024)S(1)} %get-tuple-element.24.list_ref, bf16[2048,128]{1,0:T(8,128)(2,1)S(1)} %get-tuple-element.25.mine_ref, ...), custom_call_target="tpu_custom_call", output_to_operand_aliasing={{1}: (5, {})} | custom-call | flops 2147483648 | tf_op jit(solution)/shard_map/early/pallas_call | solution.py:267
  32.7 0.0 collective-permute-done.14.refs_5_
  32.7 0.0 collective-permute-done.12.refs_3_
  32.7 0.0 collective-permute-done.10.refs_1_
  32.7 2.2 %middle.1 = (f32[1152,256]{1,0:T(8,128)S(1)}, bf16[32,128,256]{2,1,0:T(8,128)(2,1)S(1)}) custom-call(s32[5]{0:T(128)S(1)} %get-tuple-element.23.count_ref, s32[576]{0:T(1024)S(1)} %get-tuple-element.24.list_ref, bf16[2048,256]{1,0:T(8,128)(2,1)S(1)} %get-tuple-element.29.full_ref, ...), custom_call_target="tpu_custom_call", output_to_operand_aliasing={{0}: (4, {}), {1}: (5, {})} | custom-call | flops 1073741824 | tf_op jit(solution)/shard_map/middle/pallas_call | solution.py:278
  34.9 0.0 collective-permute-done.16.refs_1_
  34.9 1.5 %late.1 = (f32[1024,128]{1,0:T(8,128)S(1)}, bf16[1024,128]{1,0:T(8,128)(2,1)S(1)}, f32[1152,256]{1,0:T(8,128)S(1)}, bf16[32,128,256]{2,1,0:T(8,128)(2,1)S(1)}) custom-call(s32[5]{0:T(128)S(1)} %get-tuple-element.23.count_ref, s32[576]{0:T(1024)S(1)} %get-tuple-element.24.list_ref, ...), custom_call_target="tpu_custom_call", output_to_operand_aliasing={{2}: (5, {}), {3}: (6, {})} | custom-call | flops 2147483648 | tf_op jit(solution)/shard_map/late/pallas_call | solution.py:289
  36.4 1.7 %collective-permute-start.18 = (bf16[1024,128]{1,0:T(8,128)(2,1)S(1)}, bf16[1024,128]{1,0:T(8,128)(2,1)S(1)}, u32[]{:S(2)}, u32[]{:S(2)}) collective-permute-start(bf16[1024,128]{1,0:T(8,128)(2,1)S(1)} %get-tuple-element.40), channel_id=1, source_target_pairs={{0,16},{16,0},{1,17},{17,1},{2,18},{18,2},{3,19},{19,3},{4,20},{20... | collective-permute-start | bytes 786440 | tf_op jit(solution)/shard_map/ppermute | solution.py:300
  38.1 3.8 %second.1 = (f32[1024,128]{1,0:T(8,128)S(1)}, bf16[1024,128]{1,0:T(8,128)(2,1)S(1)}, f32[1152,256]{1,0:T(8,128)S(1)}) custom-call(s32[5]{0:T(128)S(1)} %get-tuple-element.23.count_ref, s32[576]{0:T(1024)S(1)} %get-tuple-element.24.list_ref, bf16[2048,256]{1,0:T(8,128)(2,1)S(1)} %get-tuple-element.29.full_ref, ...), custom_call_target="tpu_custom_call", output_to_operand_aliasing={{2}: (6, {})} | custom-call | flops 2147483648 | tf_op jit(solution)/shard_map/second/pallas_call | solution.py:301
  41.9 1.2 %collective-permute-start.17 = (bf16[1024,128]{1,0:T(8,128)(2,1)S(1)}, bf16[1024,128]{1,0:T(8,128)(2,1)S(1)}, u32[]{:S(2)}, u32[]{:S(2)}) collective-permute-start(bf16[1024,128]{1,0:T(8,128)(2,1)S(1)} %get-tuple-element.39), channel_id=1, source_target_pairs={{0,16},{16,0},{1,17},{17,1},{2,18},{18,2},{3,19},{19,3},{4,20},{20... | collective-permute-start | bytes 786440 | tf_op jit(solution)/shard_map/ppermute | solution.py:312
  43.1 1.5 %collective-permute-done.18.came_ref = bf16[1024,128]{1,0:T(8,128)(2,1)S(1)} collective-permute-done((bf16[1024,128]{1,0:T(8,128)(2,1)S(1)}, bf16[1024,128]{1,0:T(8,128)(2,1)S(1)}, u32[]{:S(2)}, u32[]{:S(2)}) %collective-permute-start.18) | collective-permute-done | bytes 262176 | tf_op jit(solution)/shard_map/ppermute | solution.py:300
  44.6 0.8 %shard_map.55.refs_0_ = bf16[2048,128]{1,0:T(8,128)(2,1)} custom-call(f32[1024,128]{1,0:T(8,128)S(1)} %get-tuple-element.37.__.keep_ref, bf16[1024,128]{1,0:T(8,128)(2,1)S(1)} %collective-permute-done.18.came_ref), custom_call_target="tpu_custom_call" | custom-call | tf_op jit(solution)/shard_map/pallas_call | solution.py:315
  45.4 5.0 %collective-permute-done.17.came_ref = bf16[1024,128]{1,0:T(8,128)(2,1)S(1)} collective-permute-done((bf16[1024,128]{1,0:T(8,128)(2,1)S(1)}, bf16[1024,128]{1,0:T(8,128)(2,1)S(1)}, u32[]{:S(2)}, u32[]{:S(2)}) %collective-permute-start.17) | collective-permute-done | bytes 262176 | tf_op jit(solution)/shard_map/ppermute | solution.py:312
  50.4 0.7 %shard_map.56 = bf16[2048,128]{1,0:T(8,128)(2,1)} custom-call(f32[1024,128]{1,0:T(8,128)S(1)} %get-tuple-element.38.keep_ref, bf16[1024,128]{1,0:T(8,128)(2,1)S(1)} %collective-permute-done.17.came_ref, bf16[2048,128]{1,0:T(8,128)(2,1)} %shard_map.55.refs_0_), custom_call_target="tpu_custom_call", output_to_operand_aliasing={{}: (2, {})} | custom-call | tf_op jit(solution)/shard_map/pallas_call | solution.py:315
Async XLA Ops:
  0.0 29.6 %collective-permute-start = (bf16[2048,128]{1,0:T(8,128)(2,1)}, bf16[2048,128]{1,0:T(8,128)(2,1)S(1)}, u32[]{:S(2)}, u32[]{:S(2)}) collective-permute-start(bf16[2048,128]{1,0:T(8,128)(2,1)} %mine_hbm.1), channel_id=1, source_target_pairs={{0,16},{16,0},{1,17},{17,1},{2,18},{18,2},{3,19},{19,3},{4,20},{20... | collective-permute-start | bytes 1572872 | tf_op jit(solution)/shard_map/ppermute | solution.py:220
  3.0 14.1 %collective-permute-start.2 = (bf16[256,256]{1,0:T(8,128)(2,1)}, bf16[256,256]{1,0:T(8,128)(2,1)S(1)}, u32[]{:S(2)}, u32[]{:S(2)}) collective-permute-start(bf16[256,256]{1,0:T(8,128)(2,1)} %own_hbm.1), channel_id=1, source_target_pairs={{0,2},{1,3},{2,0},{3,1},{4,6},{5,7},{6,4},{7,5},{8,10},{9,11},{10,... | collective-permute-start | bytes 393224 | tf_op jit(solution)/shard_map/ppermute | solution.py:196
  4.5 12.6 %collective-permute-start.6 = (bf16[256,256]{1,0:T(8,128)(2,1)}, bf16[256,256]{1,0:T(8,128)(2,1)S(1)}, u32[]{:S(2)}, u32[]{:S(2)}) collective-permute-start(bf16[256,256]{1,0:T(8,128)(2,1)} %own_hbm.1), channel_id=1, source_target_pairs={{0,8},{1,9},{2,10},{3,11},{4,12},{5,13},{6,14},{7,15},{8,0},{9,1},... | collective-permute-start | bytes 393224 | tf_op jit(solution)/shard_map/ppermute | solution.py:196
  7.1 10.3 %collective-permute-start.1 = (bf16[256,256]{1,0:T(8,128)(2,1)}, bf16[256,256]{1,0:T(8,128)(2,1)S(1)}, u32[]{:S(2)}, u32[]{:S(2)}) collective-permute-start(bf16[256,256]{1,0:T(8,128)(2,1)} %own_hbm.1), channel_id=1, source_target_pairs={{0,1},{1,0},{2,3},{3,2},{4,5},{5,4},{6,7},{7,6},{8,9},{9,8},{10,11... | collective-permute-start | bytes 393224 | tf_op jit(solution)/shard_map/ppermute | solution.py:196
  7.1 8.2 %copy-start = (bf16[256,256]{1,0:T(8,128)(2,1)S(1)}, bf16[256,256]{1,0:T(8,128)(2,1)}, u32[]{:S(2)}) copy-start(bf16[256,256]{1,0:T(8,128)(2,1)} %own_hbm.1) | copy-start | bytes 393220
  10.6 4.7 %collective-permute-start.8 = (f32[16,128]{1,0:T(8,128)S(1)}, f32[16,128]{1,0:T(8,128)S(1)}, u32[]{:S(2)}, u32[]{:S(2)}) collective-permute-start(f32[16,128]{1,0:T(8,128)S(1)} %get-tuple-element.30.mine_ref), channel_id=1, source_target_pairs={{0,16},{16,0},{1,17},{17,1},{2,18},{18,2},{3,19},{19,3},{4,20},{20... | collective-permute-start | bytes 24584 | tf_op jit(solution)/shard_map/ppermute | solution.py:254
  15.3 5.6 %collective-permute-start.4 = (bf16[256,256]{1,0:T(8,128)(2,1)S(1)}, bf16[256,256]{1,0:T(8,128)(2,1)S(1)}, u32[]{:S(2)}, u32[]{:S(2)}) collective-permute-start(bf16[256,256]{1,0:T(8,128)(2,1)S(1)} %copy-done), channel_id=1, source_target_pairs={{0,4},{1,5},{2,6},{3,7},{4,0},{5,1},{6,2},{7,3},{8,12},{9,13},{10,... | collective-permute-start | bytes 393224 | tf_op jit(solution)/shard_map/ppermute | solution.py:196
  17.1 3.7 %collective-permute-start.3 = (bf16[256,256]{1,0:T(8,128)(2,1)S(1)}, bf16[256,256]{1,0:T(8,128)(2,1)S(1)}, u32[]{:S(2)}, u32[]{:S(2)}) collective-permute-start(bf16[256,256]{1,0:T(8,128)(2,1)S(1)} %collective-permute-done.2.refs_2_), channel_id=1, source_target_pairs={{0,1},{1,0},{2,3},{3,2},{4,5},{5,4},{6,7},{7,6},{8,9},{9,8},{10,11... | collective-permute-start | bytes 393224 | tf_op jit(solution)/shard_map/ppermute | solution.py:196
  17.1 5.9 %collective-permute-start.13 = (bf16[256,256]{1,0:T(8,128)(2,1)S(1)}, bf16[256,256]{1,0:T(8,128)(2,1)S(1)}, u32[]{:S(2)}, u32[]{:S(2)}) collective-permute-start(bf16[256,256]{1,0:T(8,128)(2,1)S(1)} %collective-permute-done.6.refs_6_), channel_id=1, source_target_pairs={{0,4},{1,5},{2,6},{3,7},{4,0},{5,1},{6,2},{7,3},{8,12},{9,13},{10,... | collective-permute-start | bytes 393224 | tf_op jit(solution)/shard_map/ppermute | solution.py:196
  17.4 5.7 %collective-permute-start.11 = (bf16[256,256]{1,0:T(8,128)(2,1)S(1)}, bf16[256,256]{1,0:T(8,128)(2,1)S(1)}, u32[]{:S(2)}, u32[]{:S(2)}) collective-permute-start(bf16[256,256]{1,0:T(8,128)(2,1)S(1)} %collective-permute-done.6.refs_6_), channel_id=1, source_target_pairs={{0,2},{1,3},{2,0},{3,1},{4,6},{5,7},{6,4},{7,5},{8,10},{9,11},{10,... | collective-permute-start | bytes 393224 | tf_op jit(solution)/shard_map/ppermute | solution.py:196
  20.8 4.4 %collective-permute-start.7 = (bf16[256,256]{1,0:T(8,128)(2,1)S(1)}, bf16[256,256]{1,0:T(8,128)(2,1)S(1)}, u32[]{:S(2)}, u32[]{:S(2)}) collective-permute-start(bf16[256,256]{1,0:T(8,128)(2,1)S(1)} %collective-permute-done.6.refs_6_), channel_id=1, source_target_pairs={{0,1},{1,0},{2,3},{3,2},{4,5},{5,4},{6,7},{7,6},{8,9},{9,8},{10,11... | collective-permute-start | bytes 393224 | tf_op jit(solution)/shard_map/ppermute | solution.py:196
  20.8 6.4 %collective-permute-start.9 = (bf16[256,256]{1,0:T(8,128)(2,1)S(1)}, bf16[256,256]{1,0:T(8,128)(2,1)S(1)}, u32[]{:S(2)}, u32[]{:S(2)}) collective-permute-start(bf16[256,256]{1,0:T(8,128)(2,1)S(1)} %collective-permute-done.4.refs_4_), channel_id=1, source_target_pairs={{0,2},{1,3},{2,0},{3,1},{4,6},{5,7},{6,4},{7,5},{8,10},{9,11},{10,... | collective-permute-start | bytes 393224 | tf_op jit(solution)/shard_map/ppermute | solution.py:196
  23.1 4.2 %collective-permute-start.5 = (bf16[256,256]{1,0:T(8,128)(2,1)S(1)}, bf16[256,256]{1,0:T(8,128)(2,1)S(1)}, u32[]{:S(2)}, u32[]{:S(2)}) collective-permute-start(bf16[256,256]{1,0:T(8,128)(2,1)S(1)} %collective-permute-done.4.refs_4_), channel_id=1, source_target_pairs={{0,1},{1,0},{2,3},{3,2},{4,5},{5,4},{6,7},{7,6},{8,9},{9,8},{10,11... | collective-permute-start | bytes 393224 | tf_op jit(solution)/shard_map/ppermute | solution.py:196
  23.1 6.5 %collective-permute-start.15 = (bf16[256,256]{1,0:T(8,128)(2,1)S(1)}, bf16[256,256]{1,0:T(8,128)(2,1)S(1)}, u32[]{:S(2)}, u32[]{:S(2)}) collective-permute-start(bf16[256,256]{1,0:T(8,128)(2,1)S(1)} %collective-permute-done.13.refs_4_), channel_id=1, source_target_pairs={{0,2},{1,3},{2,0},{3,1},{4,6},{5,7},{6,4},{7,5},{8,10},{9,11},{10,... | collective-permute-start | bytes 393224 | tf_op jit(solution)/shard_map/ppermute | solution.py:196
  25.2 7.5 %collective-permute-start.14 = (bf16[256,256]{1,0:T(8,128)(2,1)S(1)}, bf16[256,256]{1,0:T(8,128)(2,1)S(1)}, u32[]{:S(2)}, u32[]{:S(2)}) collective-permute-start(bf16[256,256]{1,0:T(8,128)(2,1)S(1)} %collective-permute-done.13.refs_4_), channel_id=1, source_target_pairs={{0,1},{1,0},{2,3},{3,2},{4,5},{5,4},{6,7},{7,6},{8,9},{9,8},{10,11... | collective-permute-start | bytes 393224 | tf_op jit(solution)/shard_map/ppermute | solution.py:196
  27.2 5.5 %collective-permute-start.12 = (bf16[256,256]{1,0:T(8,128)(2,1)S(1)}, bf16[256,256]{1,0:T(8,128)(2,1)S(1)}, u32[]{:S(2)}, u32[]{:S(2)}) collective-permute-start(bf16[256,256]{1,0:T(8,128)(2,1)S(1)} %collective-permute-done.11.refs_2_), channel_id=1, source_target_pairs={{0,1},{1,0},{2,3},{3,2},{4,5},{5,4},{6,7},{7,6},{8,9},{9,8},{10,11... | collective-permute-start | bytes 393224 | tf_op jit(solution)/shard_map/ppermute | solution.py:196
  27.2 5.5 %collective-permute-start.10 = (bf16[256,256]{1,0:T(8,128)(2,1)S(1)}, bf16[256,256]{1,0:T(8,128)(2,1)S(1)}, u32[]{:S(2)}, u32[]{:S(2)}) collective-permute-start(bf16[256,256]{1,0:T(8,128)(2,1)S(1)} %collective-permute-done.9.refs_0_), channel_id=1, source_target_pairs={{0,1},{1,0},{2,3},{3,2},{4,5},{5,4},{6,7},{7,6},{8,9},{9,8},{10,11... | collective-permute-start | bytes 393224 | tf_op jit(solution)/shard_map/ppermute | solution.py:196
  29.6 5.3 %collective-permute-start.16 = (bf16[256,256]{1,0:T(8,128)(2,1)S(1)}, bf16[256,256]{1,0:T(8,128)(2,1)S(1)}, u32[]{:S(2)}, u32[]{:S(2)}) collective-permute-start(bf16[256,256]{1,0:T(8,128)(2,1)S(1)} %collective-permute-done.15.refs_0_), channel_id=1, source_target_pairs={{0,1},{1,0},{2,3},{3,2},{4,5},{5,4},{6,7},{7,6},{8,9},{9,8},{10,11... | collective-permute-start | bytes 393224 | tf_op jit(solution)/shard_map/ppermute | solution.py:196
  36.4 8.2 %collective-permute-start.18 = (bf16[1024,128]{1,0:T(8,128)(2,1)S(1)}, bf16[1024,128]{1,0:T(8,128)(2,1)S(1)}, u32[]{:S(2)}, u32[]{:S(2)}) collective-permute-start(bf16[1024,128]{1,0:T(8,128)(2,1)S(1)} %get-tuple-element.40), channel_id=1, source_target_pairs={{0,16},{16,0},{1,17},{17,1},{2,18},{18,2},{3,19},{19,3},{4,20},{20... | collective-permute-start | bytes 786440 | tf_op jit(solution)/shard_map/ppermute | solution.py:300
  41.9 8.5 %collective-permute-start.17 = (bf16[1024,128]{1,0:T(8,128)(2,1)S(1)}, bf16[1024,128]{1,0:T(8,128)(2,1)S(1)}, u32[]{:S(2)}, u32[]{:S(2)}) collective-permute-start(bf16[1024,128]{1,0:T(8,128)(2,1)S(1)} %get-tuple-element.39), channel_id=1, source_target_pairs={{0,16},{16,0},{1,17},{17,1},{2,18},{18,2},{3,19},{19,3},{4,20},{20... | collective-permute-start | bytes 786440 | tf_op jit(solution)/shard_map/ppermute | solution.py:312
